TPU v7x, 32 devices: a whole 2x2x4 slice. The times are simulated.
32 devices in a mesh: section: 4 (over y, core), tp: 8 (over z, x).
Axes of the slice: x: 2, y: 2, z: 4, core: 2. Of those that a mesh axis runs over, the one named last changes fastest.
Arguments:
- section_inputs: bfloat16 [4, 2, 64, 8192], P('section', None, 'tp'), may hold values from -6 to 6
- norm_gain: bfloat16 [4, 8192], P('section'), may hold values from 0.5 to 1.5
- w_query: bfloat16 [4, 8192, 4096], P('section', None, 'tp'), may hold values from -0.0625 to 0.0625
- key_projection: bfloat16 [4, 8192, 512], P('section', 'tp'), may hold values from -0.0625 to 0.0625
- value_projection: bfloat16 [4, 8192, 512], P('section', 'tp'), may hold values from -0.0625 to 0.0625
- w_out: bfloat16 [4, 4096, 8192], P('section', 'tp'), may hold values from -0.09375 to 0.09375
- token_dir: bfloat16 [2, 64, 8192], P(None, 'tp'), may hold values from -6 to 6
- tok_logratio: float32 [2, 64], P(None, 'tp'), may hold values from -4 to 4
- segment_ids: int32 [2, 64], replicated, may hold values from 0 to 7, as said below
- pair_of_slot: int32 [2, 4], replicated, may hold values from 0 to 7, as said below
- pair_counts: int32 [8, 2], replicated, may hold values from 1 to 24, as said below
Outputs:
- input_grads: bfloat16 [4, 2, 64, 8192], P('section', None, 'tp')
- grad_w_query: bfloat16 [4, 8192, 4096], P('section', None, 'tp')
- grad_w_key: bfloat16 [4, 8192, 512], P('section', 'tp')
- grad_w_value: bfloat16 [4, 8192, 512], P('section', 'tp')
- grad_w_out: bfloat16 [4, 4096, 8192], P('section', 'tp')
- grad_norm_gain: float32 [4, 8192], P('section')
Inputs may be any that keep to these rules, and one draw needn't show every extreme that they name: `segment_ids`: in each micro-batch the segment ids do not fall along the tokens and take every value of 0 to 7; segment 2 j is the chosen and 2 j + 1 the rejected sequence of slot j; each sequence has 1 to 24 tokens and one of each micro-batch has exactly 24. `pair_of_slot`: every pair stands in exactly one slot. pair_counts[p] holds the token counts of the chosen and the rejected sequence of pair p as they stand in segment_ids.
All inputs are finite; a program needn't handle non-finite values.
Results may differ from a plain program's by a relative error of at most 0.038.
Values may be sent and summed in bfloat16 or wider, within the bound.
A program may use at most 192 MiB of HBM per device.

v0:
```python
import functools
import math

import jax
import jax.numpy as jnp
from jax import lax
from jax.experimental import pallas as pl
from jax.experimental.pallas import tpu as pltpu
from jax.sharding import PartitionSpec as P

HEAD_WIDTH = 128
SLOTS = 4
LANES = 128

norm_epsilon = 1e-05
pair_beta = 4.0
masked_score = -1e30

MESH = pl.DeviceIdType.MESH
VMEM_LIMIT = 56 * 1024 * 1024
low, wide = jnp.bfloat16, jnp.float32


def contract(left, right, left_dim, right_dim):
    return lax.dot_general(
        left, right, (((left_dim,), (right_dim,)), ((), ())), preferred_element_type=wide
    )


def inner_size(tp_count):
    inner = 1
    while 2 * (2 * inner) ** 2 <= tp_count:
        inner *= 2
    return inner


def relay_kernel(
    section_count,
    tp_count,
    saved_ref,
    gain_ref,
    wq_hbm,
    kw_hbm,
    vw_hbm,
    wo_hbm,
    dir_ref,
    sums_ref,
    counts_ref,
    member_ref,
    allowed_ref,
    gin_ref,
    up_ref,
    normed_ref,
    att_ref,
    gq_ref,
    dkv_ref,
    gain_out_ref,
    wq,
    kw,
    vw,
    wo,
    nall,
    gall,
    part,
    near_recv,
    far_send,
    far_recv,
    unit,
    inverse,
    grad_unit,
    queries,
    kv,
    kv_part,
    kv_far,
    kv_near,
    probs,
    grad_heads,
    key_add,
    dkv_near,
    dkv_far,
    sums_all,
    gain_all,
    w_sem,
    s_send,
    s_recv,
    nf_send,
    nf_recv,
    nn_send,
    nn_recv,
    gf_send,
    gf_recv,
    gn_send,
    gn_recv,
    hop_send,
    kf_send,
    kf_recv,
    kn_send,
    kn_recv,
    dn_send,
    dn_recv,
    df_send,
    df_recv,
    pn_send,
    pn_recv,
    pf_send,
    pf_recv,
    t_send,
    t_recv,
):
    sec = lax.axis_index("section")
    me = lax.axis_index("tp")
    inner = inner_size(tp_count)
    outer = tp_count // inner
    z, x = me // inner, lax.rem(me, inner)
    batch_groups, rows, width = saved_ref.shape
    tokens = rows * tp_count
    every = batch_groups * tokens
    head_cols = wq.shape[1]
    local_heads = head_cols // HEAD_WIDTH
    slice_width, key_width = kw.shape
    key_count = key_width // HEAD_WIDTH
    sharers = tp_count // key_count
    group_width = inner * slice_width
    step_width = min(1024, group_width)
    scale = 1.0 / math.sqrt(HEAD_WIDTH)
    is_last = sec == section_count - 1
    feeds = sec > 0

    def zpeer(zd):
        return lax.rem(z + zd, outer)

    def xpeer(xd):
        return lax.rem(x + xd, inner)

    def remote(source, target, send, receive, section, index):
        return pltpu.make_async_remote_copy(
            src_ref=source,
            dst_ref=target,
            send_sem=send,
            recv_sem=receive,
            device_id=(section, index),
            device_id_type=MESH,
        )

    def far(source, target, send, receive, zd):
        return remote(source, target, send, receive, sec, zpeer(zd) * inner + x)

    def near(source, target, send, receive, xd):
        return remote(source, target, send, receive, sec, z * inner + xpeer(xd))

    def columns(start, size):
        return pl.ds(pl.multiple_of(start, HEAD_WIDTH), size)

    loads = [
        pltpu.make_async_copy(source, target, w_sem.at[i])
        for i, (source, target) in enumerate(
            ((kw_hbm, kw), (vw_hbm, vw), (wq_hbm, wq), (wo_hbm, wo))
        )
    ]
    for load in loads:
        load.start()

    barrier = pltpu.get_barrier_semaphore()
    for d in range(1, tp_count):
        pl.semaphore_signal(
            barrier, inc=1, device_id=(sec, lax.rem(me + d, tp_count)), device_id_type=MESH
        )

    @pl.when(sec < section_count - 1)
    def _():
        for zd in range(outer):
            pl.semaphore_signal(
                barrier, inc=1, device_id=(sec + 1, zpeer(zd) * inner + x), device_id_type=MESH
            )

    gain_row = gain_ref[...].astype(wide)
    for m in range(batch_groups):
        rows_in = saved_ref[m].astype(wide)
        inv = lax.rsqrt(jnp.mean(rows_in * rows_in, -1, keepdims=True) + norm_epsilon)
        inverse[m] = jnp.broadcast_to(inv, (rows, LANES))
        unit_rows = rows_in * inv
        unit[m] = unit_rows
        nall[me, m] = (unit_rows * gain_row).astype(low)

    @pl.when(feeds)
    def _():
        pl.semaphore_wait(barrier, tp_count - 1 + outer)

    @pl.when(jnp.logical_not(feeds))
    def _():
        pl.semaphore_wait(barrier, tp_count - 1)

    def sums_copy(d):
        return remote(
            sums_ref, sums_all.at[me], s_send.at[d], s_recv.at[d], sec, lax.rem(me + d, tp_count)
        )

    def block_from(zd):
        return lax.rem(z - zd + outer, outer) * inner + x

    def normed_far(zd):
        return far(nall.at[me], nall.at[me], nf_send.at[zd], nf_recv.at[zd], zd)

    def normed_near(zd, xd):
        block = nall.at[block_from(zd)]
        slot = zd * inner + xd
        return near(block, block, nn_send.at[slot], nn_recv.at[slot], xd)

    def top_far(m, zd):
        return far(gall.at[m, me], gall.at[m, me], gf_send.at[m, zd], gf_recv.at[m, zd], zd)

    def hop(m, zd, section):
        return remote(
            gin_ref.at[m],
            gall.at[m, me],
            hop_send.at[m, zd],
            gf_recv.at[m, zd],
            section,
            zpeer(zd) * inner + x,
        )

    def grad_near(m, zd, xd):
        block = gall.at[m, block_from(zd)]
        slot = zd * inner + xd
        return near(block, block, gn_send.at[m, slot], gn_recv.at[m, slot], xd)

    def top_forward(m):
        for zd in range(1, outer):
            top_far(m, zd).wait()
            for xd in range(1, inner):
                grad_near(m, zd, xd).start()

    @pl.when(is_last)
    def _():
        for d in range(1, tp_count):
            sums_copy(d).start()
        sums_all[me] = sums_ref[...]

    for zd in range(1, outer):
        normed_far(zd).start()
    for xd in range(1, inner):
        normed_near(0, xd).start()

    @pl.when(is_last)
    def _():
        for d in range(1, tp_count):
            sums_copy(d).wait()
        total = sums_all[0]
        for d in range(1, tp_count):
            total = total + sums_all[d]
        chosen, rejected = counts_ref[0:1], counts_ref[1:2]
        margin = pair_beta * (total[0:1] / chosen - total[1:2] / rejected)
        weight = pair_beta * jax.nn.sigmoid(-margin)
        for m in range(batch_groups):
            token_weight = jnp.sum(
                member_ref[0, m] * (-weight / chosen) + member_ref[1, m] * (weight / rejected),
                -1,
                keepdims=True,
            )
            gall[m, me] = (token_weight * dir_ref[m].astype(wide)).astype(low)
            for zd in range(1, outer):
                top_far(m, zd).start()
            for xd in range(1, inner):
                grad_near(m, 0, xd).start()

    for zd in range(1, outer):
        normed_far(zd).wait()
        for xd in range(1, inner):
            normed_near(zd, xd).start()
    for zd in range(outer):
        for xd in range(1, inner):
            normed_near(zd, xd).wait()

    pl.when(is_last)(functools.partial(top_forward, 0))

    def merge(k, carry):
        cols = columns(k * step_width, step_width)
        for m in range(batch_groups):
            normed_ref[m * tokens : (m + 1) * tokens, cols] = jnp.concatenate(
                [nall[j, m, :, cols].astype(wide) for j in range(tp_count)], 0
            ).astype(low)
        return carry

    lax.fori_loop(0, width // step_width, merge, 0)

    own_slice = columns(me * slice_width, slice_width)
    loads[0].wait()
    loads[1].wait()
    for kind, weight_ref in enumerate((kw, vw)):
        product = jnp.dot(normed_ref[:, own_slice], weight_ref[...], preferred_element_type=wide)
        for k in range(key_count):
            kv_part[k, kind] = product[:, k * HEAD_WIDTH : (k + 1) * HEAD_WIDTH].astype(low)

    def kv_far_copy(zd):
        head = zpeer(zd) * inner // sharers
        return far(kv_part.at[head], kv_far.at[zd], kf_send.at[zd], kf_recv.at[zd], zd)

    def kv_near_copy(xd):
        return near(kv_near.at[0], kv_near.at[xd], kn_send.at[xd], kn_recv.at[xd], xd)

    for zd in range(1, outer):
        kv_far_copy(zd).start()

    loads[2].wait()

    def project(k, total):
        cols = columns(k * step_width, step_width)
        return total + jnp.dot(normed_ref[:, cols], wq[cols, :], preferred_element_type=wide)

    product = lax.fori_loop(
        0, width // step_width, project, jnp.zeros((every, head_cols), wide)
    ).astype(low)
    for m in range(batch_groups):
        queries[m] = product[m * tokens : (m + 1) * tokens]

    pl.when(is_last)(functools.partial(top_forward, 1))

    for zd in range(1, outer):
        kv_far_copy(zd).wait()
    for kind in range(2):
        total = kv_part[z * inner // sharers, kind].astype(wide)
        for zd in range(1, outer):
            total = total + kv_far[zd, kind].astype(wide)
        kv_near[0, kind] = total.astype(low)
    for xd in range(1, inner):
        kv_near_copy(xd).start()
    for xd in range(1, inner):
        kv_near_copy(xd).wait()
    for kind in range(2):
        total = kv_near[0, kind].astype(wide)
        for xd in range(1, inner):
            total = total + kv_near[xd, kind].astype(wide)
        total = total.astype(low)
        for m in range(batch_groups):
            kv[m, kind] = total[m * tokens : (m + 1) * tokens]

    for m in range(batch_groups):
        mask = allowed_ref[m] > 0.5
        for h in range(local_heads):
            head = slice(h * HEAD_WIDTH, (h + 1) * HEAD_WIDTH)
            scores = contract(queries[m, :, head], kv[m, 0], 1, 1) * scale
            value = jnp.exp(jnp.where(mask, scores, masked_score))
            value = value / jnp.sum(value, -1, keepdims=True)
            probs[m, h] = value
            att_ref[m * tokens : (m + 1) * tokens, head] = jnp.dot(
                value.astype(low), kv[m, 1], preferred_element_type=wide
            ).astype(low)
    loads[3].wait()
    gain_out_ref[...] = jnp.zeros_like(gain_out_ref)
    key_add[...] = jnp.zeros_like(key_add)

    def dkv_near_copy(m, xd):
        return near(
            dkv_near.at[m, 0], dkv_near.at[m, xd], dn_send.at[m, xd], dn_recv.at[m, xd], xd
        )

    def dkv_far_copy(m, zd):
        block = dkv_far.at[m, z]
        return far(block, block, df_send.at[m, zd], df_recv.at[m, zd], zd)

    def group(i):
        return columns(lax.rem(z + i, outer) * group_width, group_width)

    def part_near(m, i, xd):
        return near(
            part.at[m, xpeer(xd), :, :, group(i)],
            near_recv.at[m, xd - 1, :, :, group(i)],
            pn_send.at[m, xd, i - 1],
            pn_recv.at[m, xd, i - 1],
            xd,
        )

    def part_far(m, i, c, zd):
        cols = columns(c * group_width, group_width)
        return far(
            far_send.at[m, zd, :, cols],
            far_recv.at[m, zd, :, cols],
            pf_send.at[m, zd, i - 1],
            pf_recv.at[m, zd, i - 1],
            zd,
        )

    def part_group(m, i, with_keys):
        base = lax.rem(z + i, outer) * group_width

        def piece(k, carry):
            start = base + k * step_width
            cols = columns(start, step_width)
            product = contract(gq_ref[m], wq[cols, :], 1, 1)
            if with_keys:
                product = product + key_add[:, columns(k * step_width, step_width)]
            for block in range(tp_count):
                part[m, block % inner, block // inner, :, cols] = product[
                    block * rows : (block + 1) * rows
                ].astype(low)
            return carry

        lax.fori_loop(0, group_width // step_width, piece, 0)
        for xd in range(1, inner):
            part_near(m, i, xd).start()

    def sum_group(m, i):
        cols = group(i)
        for xd in range(1, inner):
            part_near(m, i, xd).wait()
        for zd in range(outer):
            total = part[m, x, zpeer(zd), :, cols].astype(wide)
            for xd in range(1, inner):
                total = total + near_recv[m, xd - 1, zpeer(zd), :, cols].astype(wide)
            if zd:
                far_send[m, zd, :, cols] = total.astype(low)
                part_far(m, i, lax.rem(z + i, outer), zd).start()
            else:
                far_recv[m, 0, :, cols] = total.astype(low)

    def step(m, carry):
        @pl.when(jnp.logical_not(is_last))
        def _():
            for zd in range(outer):
                hop(m, zd, sec).wait_recv()
                for xd in range(1, inner):
                    grad_near(m, zd, xd).start()

        for zd in range(outer):
            for xd in range(1, inner):
                grad_near(m, zd, xd).wait()

        def upstream(k, total):
            cols = columns(k * step_width, step_width)
            piece = jnp.concatenate(
                [gall[m, j, :, cols].astype(wide) for j in range(tp_count)], 0
            ).astype(low)
            up_ref[m, :, cols] = piece
            return total + contract(piece, wo[:, cols], 1, 1)

        grad_heads[...] = lax.fori_loop(
            0, width // step_width, upstream, jnp.zeros((tokens, head_cols), wide)
        ).astype(low)
        grad_keys = jnp.zeros((tokens, HEAD_WIDTH), wide)
        grad_values = jnp.zeros((tokens, HEAD_WIDTH), wide)
        for h in range(local_heads):
            head = slice(h * HEAD_WIDTH, (h + 1) * HEAD_WIDTH)
            grad_head = grad_heads[:, head]
            prob = probs[m, h]
            grad_probs = contract(grad_head, kv[m, 1], 1, 1)
            grad_scores = prob * (grad_probs - jnp.sum(prob * grad_probs, -1, keepdims=True))
            scores_low = (grad_scores * scale).astype(low)
            gq_ref[m, :, head] = jnp.dot(
                scores_low, kv[m, 0], preferred_element_type=wide
            ).astype(low)
            grad_keys = grad_keys + contract(scores_low, queries[m, :, head], 0, 0)
            grad_values = grad_values + contract(prob.astype(low), grad_head, 0, 0)
        dkv_near[m, 0, 0] = grad_keys.astype(low)
        dkv_near[m, 0, 1] = grad_values.astype(low)
        for xd in range(1, inner):
            dkv_near_copy(m, xd).start()

        part_group(m, 1, False)

        for xd in range(1, inner):
            dkv_near_copy(m, xd).wait()
        for kind in range(2):
            total = dkv_near[m, 0, kind].astype(wide)
            for xd in range(1, inner):
                total = total + dkv_near[m, xd, kind].astype(wide)
            dkv_far[m, z, kind] = total.astype(low)
        for zd in range(1, outer):
            dkv_far_copy(m, zd).start()

        def middle(i, inner_carry):
            part_group(m, i, False)
            sum_group(m, i - 1)
            return inner_carry

        lax.fori_loop(2, outer, middle, 0)

        for zd in range(1, outer):
            dkv_far_copy(m, zd).wait()
        holders = outer // key_count
        for kind in range(2):
            for k in range(key_count):
                total = dkv_far[m, k * holders, kind].astype(wide)
                for other in range(1, holders):
                    total = total + dkv_far[m, k * holders + other, kind].astype(wide)
                dkv_ref[kind, m, :, k * HEAD_WIDTH : (k + 1) * HEAD_WIDTH] = total.astype(low)
        key_add[:, columns(x * slice_width, slice_width)] = contract(
            dkv_ref[0, m], kw[...], 1, 1
        ) + contract(dkv_ref[1, m], vw[...], 1, 1)
        part_group(m, outer, True)
        sum_group(m, outer - 1)
        sum_group(m, outer)

        for zd in range(1, outer):
            for i in range(1, outer + 1):
                part_far(m, i, lax.rem(z + i, outer), zd).wait_send()
                part_far(m, i, lax.rem(z - zd + i + outer, outer), zd).wait_recv()

        dots = jnp.zeros((rows, 1), wide)
        chunk = 1024
        for k in range(width // chunk):
            cols = slice(k * chunk, (k + 1) * chunk)
            normed_grad = jnp.sum(far_recv[m, :, :, cols].astype(wide), 0)
            unit_part = unit[m, :, cols]
            gain_out_ref[:, cols] = gain_out_ref[:, cols] + jnp.sum(
                normed_grad * unit_part, 0, keepdims=True
            )
            scaled = normed_grad * gain_ref[:, cols].astype(wide)
            grad_unit[:, cols] = scaled
            dots = dots + jnp.sum(scaled * unit_part, -1, keepdims=True)
        dots = dots / width
        inv = inverse[m, :, 0:1]
        for k in range(width // chunk):
            cols = slice(k * chunk, (k + 1) * chunk)
            gin_ref[m, :, cols] = (
                gall[m, me, :, cols].astype(wide)
                + inv * (grad_unit[:, cols] - unit[m, :, cols] * dots)
            ).astype(low)

        @pl.when(feeds)
        def _():
            for zd in range(outer):
                hop(m, zd, sec - 1).start()

        return carry

    lax.fori_loop(0, batch_groups, step, 0)

    def gain_copy(d):
        return remote(
            gain_all.at[me],
            gain_all.at[me],
            t_send.at[d],
            t_recv.at[d],
            sec,
            lax.rem(me + d, tp_count),
        )

    gain_all[me] = gain_out_ref[...]
    for d in range(1, tp_count):
        gain_copy(d).start()
    for d in range(1, tp_count):
        gain_copy(d).wait()
    total = gain_all[0]
    for d in range(1, tp_count):
        total = total + gain_all[d]
    gain_out_ref[...] = total

    @pl.when(feeds)
    def _():
        for m in range(batch_groups):
            for zd in range(outer):
                hop(m, zd, sec - 1).wait_send()


def relay(saved, gain, wq, kw, vw, wo, direction, sums, counts, member, allowed):
    tp_count = lax.axis_size("tp")
    inner = inner_size(tp_count)
    outer = tp_count // inner
    batch_groups, rows, width = saved.shape
    tokens = rows * tp_count
    every = batch_groups * tokens
    head_cols = wq.shape[1]
    key_width = kw.shape[1]
    key_count = key_width // HEAD_WIDTH
    slice_width = kw.shape[0]
    vmem = pl.BlockSpec(memory_space=pltpu.VMEM)
    hbm = pl.BlockSpec(memory_space=pl.ANY)
    dma = pltpu.SemaphoreType.DMA
    groups = batch_groups
    return pl.pallas_call(
        functools.partial(relay_kernel, lax.axis_size("section"), tp_count),
        out_shape=[
            jax.ShapeDtypeStruct((groups, rows, width), low),
            jax.ShapeDtypeStruct((groups, tokens, width), low),
            jax.ShapeDtypeStruct((every, width), low),
            jax.ShapeDtypeStruct((every, head_cols), low),
            jax.ShapeDtypeStruct((groups, tokens, head_cols), low),
            jax.ShapeDtypeStruct((2, groups, tokens, key_width), low),
            jax.ShapeDtypeStruct((1, width), wide),
        ],
        in_specs=[vmem, vmem, hbm, hbm, hbm, hbm] + [vmem] * 5,
        out_specs=[vmem] * 7,
        scratch_shapes=[
            pltpu.VMEM(wq.shape, low),
            pltpu.VMEM(kw.shape, low),
            pltpu.VMEM(vw.shape, low),
            pltpu.VMEM(wo.shape, low),
            pltpu.VMEM((tp_count, groups, rows, width), low),
            pltpu.VMEM((groups, tp_count, rows, width), low),
            pltpu.VMEM((groups, inner, outer, rows, width), low),
            pltpu.VMEM((groups, inner - 1, outer, rows, width), low),
            pltpu.VMEM((groups, outer, rows, width), low),
            pltpu.VMEM((groups, outer, rows, width), low),
            pltpu.VMEM((groups, rows, width), wide),
            pltpu.VMEM((groups, rows, LANES), wide),
            pltpu.VMEM((rows, width), wide),
            pltpu.VMEM((groups, tokens, head_cols), low),
            pltpu.VMEM((groups, 2, tokens, HEAD_WIDTH), low),
            pltpu.VMEM((key_count, 2, every, HEAD_WIDTH), low),
            pltpu.VMEM((outer, 2, every, HEAD_WIDTH), low),
            pltpu.VMEM((inner, 2, every, HEAD_WIDTH), low),
            pltpu.VMEM((groups, head_cols // HEAD_WIDTH, tokens, tokens), wide),
            pltpu.VMEM((tokens, head_cols), low),
            pltpu.VMEM((tokens, inner * slice_width), wide),
            pltpu.VMEM((groups, inner, 2, tokens, HEAD_WIDTH), low),
            pltpu.VMEM((groups, outer, 2, tokens, HEAD_WIDTH), low),
            pltpu.VMEM((tp_count, 8, LANES), wide),
            pltpu.VMEM((tp_count, 1, width), wide),
            dma((4,)),
            dma((tp_count,)),
            dma((tp_count,)),
            dma((outer,)),
            dma((outer,)),
            dma((tp_count,)),
            dma((tp_count,)),
            dma((groups, outer)),
            dma((groups, outer)),
            dma((groups, tp_count)),
            dma((groups, tp_count)),
            dma((groups, outer)),
            dma((outer,)),
            dma((outer,)),
            dma((inner,)),
            dma((inner,)),
            dma((groups, inner)),
            dma((groups, inner)),
            dma((groups, outer)),
            dma((groups, outer)),
            dma((groups, inner, outer)),
            dma((groups, inner, outer)),
            dma((groups, outer, outer)),
            dma((groups, outer, outer)),
            dma((tp_count,)),
            dma((tp_count,)),
        ],
        compiler_params=pltpu.CompilerParams(
            collective_id=0, has_side_effects=True, vmem_limit_bytes=VMEM_LIMIT
        ),
        name="relay",
    )(saved, gain, wq, kw, vw, wo, direction, sums, counts, member, allowed)


def body(
    section_inputs,
    norm_gain,
    w_query,
    key_projection,
    value_projection,
    w_out,
    token_dir,
    tok_logratio,
    segment_ids,
    pair_of_slot,
    pair_counts,
):
    tp_index = lax.axis_index("tp")
    saved = section_inputs[0]
    batch_groups, rows, width = saved.shape
    key_weight = key_projection[0]
    slice_width, key_width = key_weight.shape
    tokens = segment_ids.shape[1]
    every = batch_groups * tokens

    lane = jnp.arange(LANES, dtype=jnp.int32)
    own_ids = lax.dynamic_slice_in_dim(segment_ids, tp_index * rows, rows, 1)
    target = jnp.arange(batch_groups, dtype=jnp.int32)[:, None] * SLOTS + own_ids // 2
    parity = jnp.arange(2, dtype=jnp.int32)[:, None, None, None]
    member = (
        (lane == target[None, :, :, None]) & (own_ids[None, :, :, None] % 2 == parity)
    ).astype(wide)
    sums = jnp.sum(member * tok_logratio[None, :, :, None], (1, 2))
    sums = jnp.pad(sums, ((0, 6), (0, 0)))
    pairs = pair_of_slot.reshape(-1)
    table = pairs[None, :, None] == jnp.arange(pair_counts.shape[0], dtype=jnp.int32)
    counts = jnp.sum(
        jnp.where(table, pair_counts.T[:, None, :].astype(wide), 0.0), -1
    )
    counts = jnp.pad(
        counts, ((0, 6), (0, LANES - pairs.shape[0])), constant_values=1.0
    )
    position = jnp.arange(tokens, dtype=jnp.int32)
    allowed = (
        (segment_ids[:, :, None] == segment_ids[:, None, :])
        & (position[:, None] >= position[None, :])[None]
    ).astype(wide)

    grads, upstream, normed, attended, grad_queries, dkv, gain_total = relay(
        saved,
        norm_gain[0].reshape(1, width),
        w_query[0],
        key_weight,
        value_projection[0],
        w_out[0],
        token_dir,
        sums,
        counts,
        member,
        allowed,
    )
    normed_cols = lax.dynamic_slice_in_dim(normed, tp_index * slice_width, slice_width, 1)
    outer = functools.partial(
        lax.dot_general,
        dimension_numbers=(((0,), (0,)), ((), ())),
        preferred_element_type=wide,
    )
    return (
        grads[None],
        outer(normed, grad_queries.reshape(every, -1)).astype(low)[None],
        outer(normed_cols, dkv[0].reshape(every, key_width)).astype(low)[None],
        outer(normed_cols, dkv[1].reshape(every, key_width)).astype(low)[None],
        outer(attended, upstream.reshape(every, width)).astype(low)[None],
        gain_total,
    )


def solution(mesh):
    placed = (
        P("section", None, "tp", None),
        P("section", None),
        P("section", None, "tp"),
        P("section", "tp", None),
        P("section", "tp", None),
        P("section", "tp", None),
        P(None, "tp", None),
        P(None, "tp"),
        P(),
        P(),
        P(),
    )
    return jax.shard_map(
        body,
        mesh=mesh,
        in_specs=placed,
        out_specs=(
            P("section", None, "tp", None),
            P("section", None, "tp"),
            P("section", "tp", None),
            P("section", "tp", None),
            P("section", "tp", None),
            P("section", None),
        ),
        check_vma=False,
    )
```

profile of v0, /device:TPU:0, one launch (start us, length us, event | category | flops | bytes accessed | tf_op | source)
XLA Modules:
  0.0 264.0 jit_solution(4497136315525396788)
XLA Ops:
  0.6 0.8 eq.77
  1.4 0.1 iota_compare_fusion.2
  1.5 0.7 convert_bitcast_fusion
  2.2 0.1 select_reduce_fusion
  2.2 0.8 fusion.7
  3.0 0.1 iota_compare_fusion.1
  3.1 0.8 fusion.6
  3.9 0.6 pad.8.sums_ref
  4.5 0.6 pad.9.counts_ref
  5.1 0.7 and_convert_fusion.1.member_ref
  5.8 1.5 and_convert_fusion.allowed_ref
  7.2 238.0 %relay.1 = (bf16[2,8,8192]{2,1,0:T(8,128)(2,1)}, bf16[2,64,8192]{2,1,0:T(8,128)(2,1)}, bf16[128,8192]{1,0:T(8,128)(2,1)}, bf16[128,512]{1,0:T(8,128)(2,1)}, bf16...) custom-call(bf16[2,8,8192]{2,1,0:T(8,128)(2,1)} %bitcast.33, ...), custom_call_target="tpu_custom_call" | custom-call | tf_op jit(solution)/shard_map/relay/pallas_call | solution.py:570
  245.2 0.0 copy-start
  245.2 0.0 copy-start.3
  245.2 1.1 fusion.10
  246.4 2.4 fusion.2
  248.7 2.4 fusion.3
  251.1 0.0 copy-done
  251.1 0.0 copy-done.3
  251.1 0.0 copy-start.1
  251.1 0.0 copy-start.4
  251.1 5.8 %fusion = bf16[1,8192,512]{2,1,0:T(8,128)(2,1)} fusion(bf16[128,8192]{1,0:T(8,128)(2,1)S(1)} %copy-done, bf16[128,512]{1,0:T(8,128)(2,1)S(1)} %bitcast.35), kind=kOutput, calls=%fused_computation.2 | convolution fusion | flops 1077936128 | bytes 10616832 | tf_op jit(solution)/shard_map/dot_general | solution.py:708
  256.9 0.0 copy-done.1
  256.9 0.0 copy-done.4
  256.9 0.0 copy-start.2
  256.9 0.0 copy-start.5
  256.9 5.8 %fusion.1 = bf16[1,512,8192]{2,1,0:T(8,128)(2,1)} fusion(bf16[128,512]{1,0:T(8,128)(2,1)S(1)} %copy-done.4, bf16[128,8192]{1,0:T(8,128)(2,1)S(1)} %bitcast.28), kind=kOutput, calls=%fused_computation.3 | convolution fusion | flops 1077936128 | bytes 10616832 | tf_op jit(solution)/shard_map/dot_general | solution.py:711
  262.7 0.0 copy-done.2
  262.7 0.7 copy.19
  263.4 0.0 copy-done.5
  263.4 0.6 copy.20
  (3 shorter events, 0.0 us)
Async XLA Ops:
  245.2 5.9 %copy-start = (bf16[128,8192]{1,0:T(8,128)(2,1)S(1)}, bf16[128,8192]{1,0:T(8,128)(2,1)}, u32[]{:S(2)}) copy-start(bf16[128,8192]{1,0:T(8,128)(2,1)} %get-tuple-element.14) | copy-start | bytes 6291460
  245.2 5.9 %copy-start.3 = (bf16[2,64,512]{2,1,0:T(8,128)(2,1)S(1)}, bf16[2,64,512]{2,1,0:T(8,128)(2,1)}, u32[]{:S(2)}) copy-start(bf16[2,64,512]{2,1,0:T(8,128)(2,1)} %get-tuple-element.15) | copy-start | bytes 393220
  251.1 5.8 %copy-start.1 = (bf16[2,64,8192]{2,1,0:T(8,128)(2,1)S(1)}, bf16[2,64,8192]{2,1,0:T(8,128)(2,1)}, u32[]{:S(2)}) copy-start(bf16[2,64,8192]{2,1,0:T(8,128)(2,1)} %get-tuple-element.18) | copy-start | bytes 6291460
  251.1 5.8 %copy-start.4 = (bf16[128,512]{1,0:T(8,128)(2,1)S(1)}, bf16[128,512]{1,0:T(8,128)(2,1)}, u32[]{:S(2)}) copy-start(bf16[128,512]{1,0:T(8,128)(2,1)} %get-tuple-element.17) | copy-start | bytes 393220
  256.9 5.8 %copy-start.2 = (bf16[2,8,8192]{2,1,0:T(8,128)(2,1)S(1)}, bf16[2,8,8192]{2,1,0:T(8,128)(2,1)}, u32[]{:S(2)}) copy-start(bf16[2,8,8192]{2,1,0:T(8,128)(2,1)} %get-tuple-element.13) | copy-start | bytes 786436
  256.9 6.5 %copy-start.5 = (f32[1,8192]{1,0:T(1,128)S(1)}, f32[1,8192]{1,0:T(1,128)}, u32[]{:S(2)}) copy-start(f32[1,8192]{1,0:T(1,128)} %get-tuple-element.35) | copy-start | bytes 98308
where the time goes:
time: 264 us
  Pallas kernels  238 us (90%)
  matrix products  16.3 us (6%)
  other arithmetic  4.62 us (2%)
  local copies, waits for them, and re-layouts  4.44 us (2%)
    pallas_call x1, Pallas kernels, relay(): pl.pallas_call(functools.partial(relay_kernel, lax.axis_size('section'),...  238 us
    dot_general x1, matrix products, body(): outer(attended, upstream.reshape(every, width)).astype(low)[None]  5.77 us
    dot_general x1, matrix products, body(): outer(normed, grad_queries.reshape(every, -1)).astype(low)[None]  5.76 us

commit v1 on v0

--- a/solution.py
+++ b/solution.py
@@ -44,13 +44,14 @@
     vw_hbm,
     wo_hbm,
     dir_ref,
-    sums_ref,
+    ratio_ref,
+    ids_ref,
+    slot_ref,
     counts_ref,
-    member_ref,
-    allowed_ref,
     gin_ref,
     up_ref,
     normed_ref,
+    normed_cols_ref,
     att_ref,
     gq_ref,
     dkv_ref,
@@ -75,7 +76,8 @@
     kv_near,
     probs,
     grad_heads,
-    key_add,
+    key_send,
+    key_recv,
     dkv_near,
     dkv_far,
     sums_all,
@@ -104,8 +106,11 @@
     pn_recv,
     pf_send,
     pf_recv,
+    ks_send,
+    ks_recv,
     t_send,
     t_recv,
+    go,
 ):
     sec = lax.axis_index("section")
     me = lax.axis_index("tp")
@@ -190,9 +195,28 @@
     def _():
         pl.semaphore_wait(barrier, tp_count - 1)
 
+    def iota(shape, dim):
+        return lax.broadcasted_iota(jnp.int32, shape, dim)
+
+    def to_column(row, count, start):
+        span = row.shape[1]
+        pick = iota((count, span), 1) == iota((count, span), 0) + start
+        return jnp.sum(jnp.where(pick, jnp.broadcast_to(row, (count, span)), 0.0), -1, keepdims=True)
+
+    def own_member(m, kind):
+        own = to_column(ids_ref[m : m + 1].astype(wide), rows, me * rows)
+        slot = 2 * iota((rows, SLOTS), 1) + kind
+        return (own == slot.astype(wide)).astype(wide)
+
+    def slot_counts(m, kind):
+        pairs = counts_ref.shape[0]
+        table = iota((pairs, SLOTS), 0) == jnp.broadcast_to(slot_ref[m : m + 1], (pairs, SLOTS))
+        count = counts_ref[:, kind : kind + 1].astype(wide)
+        return jnp.sum(jnp.where(table, count, 0.0), 0, keepdims=True)
+
     def sums_copy(d):
         return remote(
-            sums_ref, sums_all.at[me], s_send.at[d], s_recv.at[d], sec, lax.rem(me + d, tp_count)
+            sums_all.at[me], sums_all.at[me], s_send.at[d], s_recv.at[d], sec, lax.rem(me + d, tp_count)
         )
 
     def block_from(zd):
@@ -232,14 +256,30 @@
 
     @pl.when(is_last)
     def _():
+        sums_all[me] = jnp.zeros(sums_all.shape[1:], wide)
+        for m in range(batch_groups):
+            ratio = to_column(ratio_ref[m : m + 1], rows, 0)
+            for kind in range(2):
+                sums_all[me, 2 * m + kind : 2 * m + kind + 1, 0:SLOTS] = jnp.sum(
+                    own_member(m, kind) * ratio, 0, keepdims=True
+                )
         for d in range(1, tp_count):
             sums_copy(d).start()
-        sums_all[me] = sums_ref[...]
+
+    @pl.when(sec == section_count - 2)
+    def _():
+        pl.semaphore_wait(go, 1)
 
     for zd in range(1, outer):
         normed_far(zd).start()
     for xd in range(1, inner):
         normed_near(0, xd).start()
+
+    def top_start(m):
+        for zd in range(1, outer):
+            top_far(m, zd).start()
+        for xd in range(1, inner):
+            grad_near(m, 0, xd).start()
 
     @pl.when(is_last)
     def _():
@@ -248,20 +288,20 @@
         total = sums_all[0]
         for d in range(1, tp_count):
             total = total + sums_all[d]
-        chosen, rejected = counts_ref[0:1], counts_ref[1:2]
-        margin = pair_beta * (total[0:1] / chosen - total[1:2] / rejected)
-        weight = pair_beta * jax.nn.sigmoid(-margin)
         for m in range(batch_groups):
+            chosen, rejected = slot_counts(m, 0), slot_counts(m, 1)
+            margin = pair_beta * (
+                total[2 * m : 2 * m + 1, 0:SLOTS] / chosen
+                - total[2 * m + 1 : 2 * m + 2, 0:SLOTS] / rejected
+            )
+            weight = pair_beta * jax.nn.sigmoid(-margin)
             token_weight = jnp.sum(
-                member_ref[0, m] * (-weight / chosen) + member_ref[1, m] * (weight / rejected),
+                own_member(m, 0) * (-weight / chosen) + own_member(m, 1) * (weight / rejected),
                 -1,
                 keepdims=True,
             )
             gall[m, me] = (token_weight * dir_ref[m].astype(wide)).astype(low)
-            for zd in range(1, outer):
-                top_far(m, zd).start()
-            for xd in range(1, inner):
-                grad_near(m, 0, xd).start()
+        top_start(0)
 
     for zd in range(1, outer):
         normed_far(zd).wait()
@@ -271,7 +311,13 @@
         for xd in range(1, inner):
             normed_near(zd, xd).wait()
 
-    pl.when(is_last)(functools.partial(top_forward, 0))
+    @pl.when(is_last)
+    def _():
+        top_forward(0)
+        for xd in range(1, inner):
+            for zd in range(outer):
+                grad_near(0, zd, xd).wait()
+        pl.semaphore_signal(go, inc=1, device_id=(sec - 1, me), device_id_type=MESH)
 
     def merge(k, carry):
         cols = columns(k * step_width, step_width)
@@ -283,11 +329,11 @@
 
     lax.fori_loop(0, width // step_width, merge, 0)
 
-    own_slice = columns(me * slice_width, slice_width)
+    normed_cols_ref[...] = normed_ref[:, columns(me * slice_width, slice_width)]
     loads[0].wait()
     loads[1].wait()
     for kind, weight_ref in enumerate((kw, vw)):
-        product = jnp.dot(normed_ref[:, own_slice], weight_ref[...], preferred_element_type=wide)
+        product = jnp.dot(normed_cols_ref[...], weight_ref[...], preferred_element_type=wide)
         for k in range(key_count):
             kv_part[k, kind] = product[:, k * HEAD_WIDTH : (k + 1) * HEAD_WIDTH].astype(low)
 
@@ -312,8 +358,6 @@
     ).astype(low)
     for m in range(batch_groups):
         queries[m] = product[m * tokens : (m + 1) * tokens]
-
-    pl.when(is_last)(functools.partial(top_forward, 1))
 
     for zd in range(1, outer):
         kv_far_copy(zd).wait()
@@ -326,6 +370,12 @@
         kv_near_copy(xd).start()
     for xd in range(1, inner):
         kv_near_copy(xd).wait()
+
+    @pl.when(is_last)
+    def _():
+        for m in range(1, batch_groups):
+            top_start(m)
+
     for kind in range(2):
         total = kv_near[0, kind].astype(wide)
         for xd in range(1, inner):
@@ -335,7 +385,10 @@
             kv[m, kind] = total[m * tokens : (m + 1) * tokens]
 
     for m in range(batch_groups):
-        mask = allowed_ref[m] > 0.5
+        ids = ids_ref[m : m + 1].astype(wide)
+        mask = (to_column(ids, tokens, 0) == jnp.broadcast_to(ids, (tokens, tokens))) & (
+            iota((tokens, tokens), 0) >= iota((tokens, tokens), 1)
+        )
         for h in range(local_heads):
             head = slice(h * HEAD_WIDTH, (h + 1) * HEAD_WIDTH)
             scores = contract(queries[m, :, head], kv[m, 0], 1, 1) * scale
@@ -347,7 +400,11 @@
             ).astype(low)
     loads[3].wait()
     gain_out_ref[...] = jnp.zeros_like(gain_out_ref)
-    key_add[...] = jnp.zeros_like(key_add)
+
+    @pl.when(is_last)
+    def _():
+        for m in range(1, batch_groups):
+            top_forward(m)
 
     def dkv_near_copy(m, xd):
         return near(
@@ -380,15 +437,19 @@
             zd,
         )
 
-    def part_group(m, i, with_keys):
+    def key_copy(m, d):
+        peer = lax.rem(me + d, tp_count)
+        return remote(
+            key_send.at[m, peer], key_recv.at[m, me], ks_send.at[m, d], ks_recv.at[m, d], sec, peer
+        )
+
+    def part_group(m, i):
         base = lax.rem(z + i, outer) * group_width
 
         def piece(k, carry):
             start = base + k * step_width
             cols = columns(start, step_width)
             product = contract(gq_ref[m], wq[cols, :], 1, 1)
-            if with_keys:
-                product = product + key_add[:, columns(k * step_width, step_width)]
             for block in range(tp_count):
                 part[m, block % inner, block // inner, :, cols] = product[
                     block * rows : (block + 1) * rows
@@ -421,9 +482,11 @@
                 for xd in range(1, inner):
                     grad_near(m, zd, xd).start()
 
-        for zd in range(outer):
-            for xd in range(1, inner):
-                grad_near(m, zd, xd).wait()
+        @pl.when(jnp.logical_not(is_last) | (m > 0))
+        def _():
+            for zd in range(outer):
+                for xd in range(1, inner):
+                    grad_near(m, zd, xd).wait()
 
         def upstream(k, total):
             cols = columns(k * step_width, step_width)
@@ -455,7 +518,7 @@
         for xd in range(1, inner):
             dkv_near_copy(m, xd).start()
 
-        part_group(m, 1, False)
+        part_group(m, 1)
 
         for xd in range(1, inner):
             dkv_near_copy(m, xd).wait()
@@ -468,11 +531,11 @@
             dkv_far_copy(m, zd).start()
 
         def middle(i, inner_carry):
-            part_group(m, i, False)
+            part_group(m, i)
             sum_group(m, i - 1)
             return inner_carry
 
-        lax.fori_loop(2, outer, middle, 0)
+        lax.fori_loop(2, outer + 1, middle, 0)
 
         for zd in range(1, outer):
             dkv_far_copy(m, zd).wait()
@@ -483,11 +546,14 @@
                 for other in range(1, holders):
                     total = total + dkv_far[m, k * holders + other, kind].astype(wide)
                 dkv_ref[kind, m, :, k * HEAD_WIDTH : (k + 1) * HEAD_WIDTH] = total.astype(low)
-        key_add[:, columns(x * slice_width, slice_width)] = contract(
-            dkv_ref[0, m], kw[...], 1, 1
-        ) + contract(dkv_ref[1, m], vw[...], 1, 1)
-        part_group(m, outer, True)
-        sum_group(m, outer - 1)
+        key_slice = contract(dkv_ref[0, m], kw[...], 1, 1) + contract(
+            dkv_ref[1, m], vw[...], 1, 1
+        )
+        for j in range(tp_count):
+            key_send[m, j] = key_slice[j * rows : (j + 1) * rows].astype(low)
+        for d in range(1, tp_count):
+            key_copy(m, d).start()
+        key_recv[m, me] = key_send[m, me]
         sum_group(m, outer)
 
         for zd in range(1, outer):
@@ -495,11 +561,16 @@
                 part_far(m, i, lax.rem(z + i, outer), zd).wait_send()
                 part_far(m, i, lax.rem(z - zd + i + outer, outer), zd).wait_recv()
 
+        for d in range(1, tp_count):
+            key_copy(m, d).wait()
+
         dots = jnp.zeros((rows, 1), wide)
         chunk = 1024
-        for k in range(width // chunk):
-            cols = slice(k * chunk, (k + 1) * chunk)
-            normed_grad = jnp.sum(far_recv[m, :, :, cols].astype(wide), 0)
+        for k in range(tp_count):
+            cols = slice(k * slice_width, (k + 1) * slice_width)
+            normed_grad = key_recv[m, k].astype(wide) + jnp.sum(
+                far_recv[m, :, :, cols].astype(wide), 0
+            )
             unit_part = unit[m, :, cols]
             gain_out_ref[:, cols] = gain_out_ref[:, cols] + jnp.sum(
                 normed_grad * unit_part, 0, keepdims=True
@@ -552,7 +623,7 @@
                 hop(m, zd, sec - 1).wait_send()
 
 
-def relay(saved, gain, wq, kw, vw, wo, direction, sums, counts, member, allowed):
+def relay(saved, gain, wq, kw, vw, wo, direction, ratio, ids, slots, counts):
     tp_count = lax.axis_size("tp")
     inner = inner_size(tp_count)
     outer = tp_count // inner
@@ -573,13 +644,14 @@
             jax.ShapeDtypeStruct((groups, rows, width), low),
             jax.ShapeDtypeStruct((groups, tokens, width), low),
             jax.ShapeDtypeStruct((every, width), low),
+            jax.ShapeDtypeStruct((every, slice_width), low),
             jax.ShapeDtypeStruct((every, head_cols), low),
             jax.ShapeDtypeStruct((groups, tokens, head_cols), low),
             jax.ShapeDtypeStruct((2, groups, tokens, key_width), low),
             jax.ShapeDtypeStruct((1, width), wide),
         ],
         in_specs=[vmem, vmem, hbm, hbm, hbm, hbm] + [vmem] * 5,
-        out_specs=[vmem] * 7,
+        out_specs=[vmem] * 8,
         scratch_shapes=[
             pltpu.VMEM(wq.shape, low),
             pltpu.VMEM(kw.shape, low),
@@ -601,7 +673,8 @@
             pltpu.VMEM((inner, 2, every, HEAD_WIDTH), low),
             pltpu.VMEM((groups, head_cols // HEAD_WIDTH, tokens, tokens), wide),
             pltpu.VMEM((tokens, head_cols), low),
-            pltpu.VMEM((tokens, inner * slice_width), wide),
+            pltpu.VMEM((groups, tp_count, rows, slice_width), low),
+            pltpu.VMEM((groups, tp_count, rows, slice_width), low),
             pltpu.VMEM((groups, inner, 2, tokens, HEAD_WIDTH), low),
             pltpu.VMEM((groups, outer, 2, tokens, HEAD_WIDTH), low),
             pltpu.VMEM((tp_count, 8, LANES), wide),
@@ -630,14 +703,94 @@
             dma((groups, inner, outer)),
             dma((groups, outer, outer)),
             dma((groups, outer, outer)),
+            dma((groups, tp_count)),
+            dma((groups, tp_count)),
             dma((tp_count,)),
             dma((tp_count,)),
+            pltpu.SemaphoreType.REGULAR,
         ],
         compiler_params=pltpu.CompilerParams(
             collective_id=0, has_side_effects=True, vmem_limit_bytes=VMEM_LIMIT
         ),
         name="relay",
-    )(saved, gain, wq, kw, vw, wo, direction, sums, counts, member, allowed)
+    )(saved, gain, wq, kw, vw, wo, direction, ratio, ids, slots, counts)
+
+
+def weights_kernel(
+    normed_ref,
+    normed_cols_ref,
+    gq_ref,
+    dkv_ref,
+    att_ref,
+    up_ref,
+    grads_in,
+    gain_in,
+    grads_out,
+    of_query,
+    of_key,
+    of_value,
+    of_out,
+    gain_out,
+):
+    @pl.when(pl.program_id(0) == 0)
+    def _():
+        grads_out[...] = grads_in[...]
+        gain_out[...] = gain_in[...]
+
+    of_query[...] = contract(normed_ref[...], gq_ref[...], 0, 0).astype(low)
+    of_out[...] = contract(att_ref[...], up_ref[...], 0, 0).astype(low)
+    of_key[...] = contract(normed_cols_ref[...], dkv_ref[0], 0, 0).astype(low)
+    of_value[...] = contract(normed_cols_ref[...], dkv_ref[1], 0, 0).astype(low)
+
+
+def weight_gradients(normed, normed_cols, grad_queries, dkv, attended, upstream, grads, gain):
+    every, width = normed.shape
+    head_cols = grad_queries.shape[1]
+    slice_width, key_width = normed_cols.shape[1], dkv.shape[2]
+    steps = slice_width // HEAD_WIDTH
+    part = width // steps
+
+    def whole(shape):
+        return pl.BlockSpec(shape, lambda i: (0,) * len(shape))
+
+    def lanes(shape):
+        return pl.BlockSpec(shape, lambda i: (0, i))
+
+    def above(shape):
+        return pl.BlockSpec(shape, lambda i: (i, 0))
+
+    return pl.pallas_call(
+        weights_kernel,
+        grid=(steps,),
+        out_shape=[
+            jax.ShapeDtypeStruct(grads.shape, low),
+            jax.ShapeDtypeStruct((width, head_cols), low),
+            jax.ShapeDtypeStruct((slice_width, key_width), low),
+            jax.ShapeDtypeStruct((slice_width, key_width), low),
+            jax.ShapeDtypeStruct((head_cols, width), low),
+            jax.ShapeDtypeStruct(gain.shape, wide),
+        ],
+        in_specs=[
+            lanes((every, part)),
+            lanes((every, HEAD_WIDTH)),
+            whole(grad_queries.shape),
+            whole(dkv.shape),
+            whole(attended.shape),
+            lanes((every, part)),
+            whole(grads.shape),
+            whole(gain.shape),
+        ],
+        out_specs=[
+            whole(grads.shape),
+            above((part, head_cols)),
+            above((HEAD_WIDTH, key_width)),
+            above((HEAD_WIDTH, key_width)),
+            lanes((head_cols, part)),
+            whole(gain.shape),
+        ],
+        compiler_params=pltpu.CompilerParams(vmem_limit_bytes=32 * 1024 * 1024),
+        name="weight_gradients",
+    )(normed, normed_cols, grad_queries, dkv, attended, upstream, grads, gain)
 
 
 def body(
@@ -653,62 +806,38 @@
     pair_of_slot,
     pair_counts,
 ):
-    tp_index = lax.axis_index("tp")
     saved = section_inputs[0]
-    batch_groups, rows, width = saved.shape
-    key_weight = key_projection[0]
-    slice_width, key_width = key_weight.shape
-    tokens = segment_ids.shape[1]
-    every = batch_groups * tokens
-
-    lane = jnp.arange(LANES, dtype=jnp.int32)
-    own_ids = lax.dynamic_slice_in_dim(segment_ids, tp_index * rows, rows, 1)
-    target = jnp.arange(batch_groups, dtype=jnp.int32)[:, None] * SLOTS + own_ids // 2
-    parity = jnp.arange(2, dtype=jnp.int32)[:, None, None, None]
-    member = (
-        (lane == target[None, :, :, None]) & (own_ids[None, :, :, None] % 2 == parity)
-    ).astype(wide)
-    sums = jnp.sum(member * tok_logratio[None, :, :, None], (1, 2))
-    sums = jnp.pad(sums, ((0, 6), (0, 0)))
-    pairs = pair_of_slot.reshape(-1)
-    table = pairs[None, :, None] == jnp.arange(pair_counts.shape[0], dtype=jnp.int32)
-    counts = jnp.sum(
-        jnp.where(table, pair_counts.T[:, None, :].astype(wide), 0.0), -1
-    )
-    counts = jnp.pad(
-        counts, ((0, 6), (0, LANES - pairs.shape[0])), constant_values=1.0
-    )
-    position = jnp.arange(tokens, dtype=jnp.int32)
-    allowed = (
-        (segment_ids[:, :, None] == segment_ids[:, None, :])
-        & (position[:, None] >= position[None, :])[None]
-    ).astype(wide)
-
-    grads, upstream, normed, attended, grad_queries, dkv, gain_total = relay(
+    width = saved.shape[2]
+    every = segment_ids.size
+    grads, upstream, normed, normed_cols, attended, grad_queries, dkv, gain_total = relay(
         saved,
         norm_gain[0].reshape(1, width),
         w_query[0],
-        key_weight,
+        key_projection[0],
         value_projection[0],
         w_out[0],
         token_dir,
-        sums,
-        counts,
-        member,
-        allowed,
+        tok_logratio,
+        segment_ids,
+        pair_of_slot,
+        pair_counts,
     )
-    normed_cols = lax.dynamic_slice_in_dim(normed, tp_index * slice_width, slice_width, 1)
-    outer = functools.partial(
-        lax.dot_general,
-        dimension_numbers=(((0,), (0,)), ((), ())),
-        preferred_element_type=wide,
+    grads, of_query, of_key, of_value, of_out, gain_total = weight_gradients(
+        normed,
+        normed_cols,
+        grad_queries.reshape(every, -1),
+        dkv.reshape(2, every, -1),
+        attended,
+        upstream.reshape(every, width),
+        grads,
+        gain_total,
     )
     return (
         grads[None],
-        outer(normed, grad_queries.reshape(every, -1)).astype(low)[None],
-        outer(normed_cols, dkv[0].reshape(every, key_width)).astype(low)[None],
-        outer(normed_cols, dkv[1].reshape(every, key_width)).astype(low)[None],
-        outer(attended, upstream.reshape(every, width)).astype(low)[None],
+        of_query[None],
+        of_key[None],
+        of_value[None],
+        of_out[None],
         gain_total,
     )
 

time: 264 us -> 261 us (0.989)
  matrix products: 16.3 us -> 0 us
  Pallas kernels: 238 us -> 250 us
  local copies, waits for them, and re-layouts: 4.44 us -> 9.93 us
  other arithmetic: 4.62 us -> 0 us
    dot_general x4 -> x0, matrix products: 16.3 us -> none  [the longest x1 5.77 us: body(): outer(attended, upstream.reshape(every, width)).astype(low)[None]]
    unnamed x14 -> x17, local copies, waits for them, and re-layouts: 1.34 us -> 9.93 us
    pallas_call x0 -> x1, Pallas kernels: none -> 8.56 us  [weight_gradients(): pl.pallas_call(weights_kernel, grid=(steps,), out_shape=[jax.ShapeDtypeSt...]
    pallas_call x1, Pallas kernels: 238 us -> 241 us  [relay(): pl.pallas_call(functools.partial(relay_kernel, lax.axis_size('section'),...]
    convert_element_type x3 -> x0, other arithmetic: 2.83 us -> none  [the longest x1 1.47 us: body(): allowed = ((segment_ids[:, :, None] == segment_ids[:, None, :]) & (positi...]
where the time goes in v1:
time: 261 us; the launch traced here: 260 us
  Pallas kernels  250 us (96%)
  local copies, waits for them, and re-layouts  9.93 us (4%)
    pallas_call x1, Pallas kernels, relay(): pl.pallas_call(functools.partial(relay_kernel, lax.axis_size('section'),...  241 us
    unnamed x17, local copies, waits for them, and re-layouts  9.93 us
    pallas_call x1, Pallas kernels, weight_gradients(): pl.pallas_call(weights_kernel, grid=(steps,), out_shape=[jax.ShapeDtypeSt...  8.56 us

profile of v1, /device:TPU:0, one launch (start us, length us, event | category | flops | bytes accessed | tf_op | source)
XLA Modules:
  0.0 260.2 jit_solution(7975987199653614736)
XLA Ops:
  0.6 1.3 copy.17.counts_ref
  2.0 241.0 %relay.1 = (bf16[2,8,8192]{2,1,0:T(8,128)(2,1)}, bf16[2,64,8192]{2,1,0:T(8,128)(2,1)}, bf16[128,8192]{1,0:T(8,128)(2,1)}, bf16[128,1024]{1,0:T(8,128)(2,1)}, bf1...) custom-call(bf16[2,8,8192]{2,1,0:T(8,128)(2,1)} %bitcast.20, ...), custom_call_target="tpu_custom_call" | custom-call | tf_op jit(solution)/shard_map/relay/pallas_call | solution.py:641
  243.0 0.0 copy-start
  243.0 1.6 copy-done
  244.6 0.0 copy-start.1
  244.6 1.6 copy-done.1
  246.2 0.0 copy-start.2
  246.2 0.9 copy-done.2
  247.1 0.0 copy-start.3
  247.1 0.9 copy-done.3
  248.1 0.0 copy-start.4
  248.1 0.9 copy-done.4
  249.0 0.0 copy-start.5
  249.0 0.9 copy-done.5
  249.9 0.0 copy-start.6
  249.9 0.9 copy-done.6
  250.8 0.0 copy-start.7
  250.8 0.8 copy-done.7
  251.6 8.6 %weight_gradients.1 = (bf16[2,8,8192]{2,1,0:T(8,128)(2,1)}, bf16[8192,512]{1,0:T(8,128)(2,1)}, bf16[1024,512]{1,0:T(8,128)(2,1)}, bf16[1024,512]{1,0:T(8,128)(2,...) custom-call(bf16[128,8192]{1,0:T(8,128)(2,1)S(1)} %copy-done.1, bf16[128,1024]{1,0:T(8,128)(2,1)S(1)} %copy-done.3, ...), custom_call_target="tpu_custom_call" | custom-call | tf_op jit(solution)/shard_map/weight_gradients/pallas_call | solution.py:762
Async XLA Ops:
  243.0 1.6 copy-start
  244.6 1.6 copy-start.1
  246.2 0.9 copy-start.2
  247.1 0.9 copy-start.3
  248.1 0.9 copy-start.4
  249.0 0.9 copy-start.5
  249.9 0.9 copy-start.6
  250.8 0.8 copy-start.7

commit v2 on v1

--- a/solution.py
+++ b/solution.py
@@ -11,13 +11,14 @@
 HEAD_WIDTH = 128
 SLOTS = 4
 LANES = 128
+CHUNKS = 4
 
 norm_epsilon = 1e-05
 pair_beta = 4.0
 masked_score = -1e30
 
 MESH = pl.DeviceIdType.MESH
-VMEM_LIMIT = 56 * 1024 * 1024
+VMEM_LIMIT = 38 * 1024 * 1024
 low, wide = jnp.bfloat16, jnp.float32
 
 
@@ -40,8 +41,8 @@
     saved_ref,
     gain_ref,
     wq_hbm,
-    kw_hbm,
-    vw_hbm,
+    kw,
+    vw,
     wo_hbm,
     dir_ref,
     ratio_ref,
@@ -57,8 +58,6 @@
     dkv_ref,
     gain_out_ref,
     wq,
-    kw,
-    vw,
     wo,
     nall,
     gall,
@@ -127,6 +126,9 @@
     sharers = tp_count // key_count
     group_width = inner * slice_width
     step_width = min(1024, group_width)
+    chunk_width = width // CHUNKS
+    per_group = CHUNKS // batch_groups
+    normed_width = width // per_group
     scale = 1.0 / math.sqrt(HEAD_WIDTH)
     is_last = sec == section_count - 1
     feeds = sec > 0
@@ -159,7 +161,7 @@
     loads = [
         pltpu.make_async_copy(source, target, w_sem.at[i])
         for i, (source, target) in enumerate(
-            ((kw_hbm, kw), (vw_hbm, vw), (wq_hbm, wq), (wo_hbm, wo))
+            ((wq_hbm, wq), (wo_hbm, wo))
         )
     ]
     for load in loads:
@@ -222,37 +224,47 @@
     def block_from(zd):
         return lax.rem(z - zd + outer, outer) * inner + x
 
-    def normed_far(zd):
-        return far(nall.at[me], nall.at[me], nf_send.at[zd], nf_recv.at[zd], zd)
-
-    def normed_near(zd, xd):
-        block = nall.at[block_from(zd)]
+    def normed_piece(block, c):
+        start = c % per_group * normed_width
+        return nall.at[block, c // per_group, :, start : start + normed_width]
+
+    def normed_far(c, zd):
+        block = normed_piece(me, c)
+        return far(block, block, nf_send.at[c, zd], nf_recv.at[c, zd], zd)
+
+    def normed_near(c, zd, xd):
+        block = normed_piece(block_from(zd), c)
         slot = zd * inner + xd
-        return near(block, block, nn_send.at[slot], nn_recv.at[slot], xd)
-
-    def top_far(m, zd):
-        return far(gall.at[m, me], gall.at[m, me], gf_send.at[m, zd], gf_recv.at[m, zd], zd)
-
-    def hop(m, zd, section):
+        return near(block, block, nn_send.at[c, slot], nn_recv.at[c, slot], xd)
+
+    def chunk(c):
+        return columns(c * chunk_width, chunk_width)
+
+    def top_far(m, c, zd):
+        block = gall.at[m, me, :, chunk(c)]
+        return far(block, block, gf_send.at[m, c, zd], gf_recv.at[m, c, zd], zd)
+
+    def hop(m, c, zd, section):
         return remote(
-            gin_ref.at[m],
-            gall.at[m, me],
-            hop_send.at[m, zd],
-            gf_recv.at[m, zd],
+            gin_ref.at[m, :, chunk(c)],
+            gall.at[m, me, :, chunk(c)],
+            hop_send.at[m, c, zd],
+            gf_recv.at[m, c, zd],
             section,
             zpeer(zd) * inner + x,
         )
 
-    def grad_near(m, zd, xd):
-        block = gall.at[m, block_from(zd)]
+    def grad_near(m, c, zd, xd):
+        block = gall.at[m, block_from(zd), :, chunk(c)]
         slot = zd * inner + xd
-        return near(block, block, gn_send.at[m, slot], gn_recv.at[m, slot], xd)
+        return near(block, block, gn_send.at[m, c, slot], gn_recv.at[m, c, slot], xd)
 
     def top_forward(m):
-        for zd in range(1, outer):
-            top_far(m, zd).wait()
-            for xd in range(1, inner):
-                grad_near(m, zd, xd).start()
+        for c in range(CHUNKS):
+            for zd in range(1, outer):
+                top_far(m, c, zd).wait()
+                for xd in range(1, inner):
+                    grad_near(m, c, zd, xd).start()
 
     @pl.when(is_last)
     def _():
@@ -270,16 +282,18 @@
     def _():
         pl.semaphore_wait(go, 1)
 
-    for zd in range(1, outer):
-        normed_far(zd).start()
-    for xd in range(1, inner):
-        normed_near(0, xd).start()
+    for c in range(CHUNKS):
+        for zd in range(1, outer):
+            normed_far(c, zd).start()
+        for xd in range(1, inner):
+            normed_near(c, 0, xd).start()
 
     def top_start(m):
-        for zd in range(1, outer):
-            top_far(m, zd).start()
-        for xd in range(1, inner):
-            grad_near(m, 0, xd).start()
+        for c in range(CHUNKS):
+            for zd in range(1, outer):
+                top_far(m, c, zd).start()
+            for xd in range(1, inner):
+                grad_near(m, c, 0, xd).start()
 
     @pl.when(is_last)
     def _():
@@ -303,20 +317,19 @@
             gall[m, me] = (token_weight * dir_ref[m].astype(wide)).astype(low)
         top_start(0)
 
-    for zd in range(1, outer):
-        normed_far(zd).wait()
-        for xd in range(1, inner):
-            normed_near(zd, xd).start()
-    for zd in range(outer):
-        for xd in range(1, inner):
-            normed_near(zd, xd).wait()
+    for c in range(CHUNKS):
+        for zd in range(1, outer):
+            normed_far(c, zd).wait()
+            for xd in range(1, inner):
+                normed_near(c, zd, xd).start()
+    for c in range(CHUNKS):
+        for zd in range(outer):
+            for xd in range(1, inner):
+                normed_near(c, zd, xd).wait()
 
     @pl.when(is_last)
     def _():
         top_forward(0)
-        for xd in range(1, inner):
-            for zd in range(outer):
-                grad_near(0, zd, xd).wait()
         pl.semaphore_signal(go, inc=1, device_id=(sec - 1, me), device_id_type=MESH)
 
     def merge(k, carry):
@@ -330,8 +343,6 @@
     lax.fori_loop(0, width // step_width, merge, 0)
 
     normed_cols_ref[...] = normed_ref[:, columns(me * slice_width, slice_width)]
-    loads[0].wait()
-    loads[1].wait()
     for kind, weight_ref in enumerate((kw, vw)):
         product = jnp.dot(normed_cols_ref[...], weight_ref[...], preferred_element_type=wide)
         for k in range(key_count):
@@ -347,7 +358,7 @@
     for zd in range(1, outer):
         kv_far_copy(zd).start()
 
-    loads[2].wait()
+    loads[0].wait()
 
     def project(k, total):
         cols = columns(k * step_width, step_width)
@@ -398,7 +409,7 @@
             att_ref[m * tokens : (m + 1) * tokens, head] = jnp.dot(
                 value.astype(low), kv[m, 1], preferred_element_type=wide
             ).astype(low)
-    loads[3].wait()
+    loads[1].wait()
     gain_out_ref[...] = jnp.zeros_like(gain_out_ref)
 
     @pl.when(is_last)
@@ -475,29 +486,32 @@
                 far_recv[m, 0, :, cols] = total.astype(low)
 
     def step(m, carry):
-        @pl.when(jnp.logical_not(is_last))
-        def _():
-            for zd in range(outer):
-                hop(m, zd, sec).wait_recv()
-                for xd in range(1, inner):
-                    grad_near(m, zd, xd).start()
-
-        @pl.when(jnp.logical_not(is_last) | (m > 0))
-        def _():
+        def forward(c):
+            @pl.when(jnp.logical_not(is_last))
+            def _():
+                for zd in range(outer):
+                    hop(m, c, zd, sec).wait_recv()
+                    for xd in range(1, inner):
+                        grad_near(m, c, zd, xd).start()
+
+        forward(0)
+
+        def upstream(c, total):
+            pl.when(c + 1 < CHUNKS)(functools.partial(forward, c + 1))
             for zd in range(outer):
                 for xd in range(1, inner):
-                    grad_near(m, zd, xd).wait()
-
-        def upstream(k, total):
-            cols = columns(k * step_width, step_width)
-            piece = jnp.concatenate(
-                [gall[m, j, :, cols].astype(wide) for j in range(tp_count)], 0
-            ).astype(low)
-            up_ref[m, :, cols] = piece
-            return total + contract(piece, wo[:, cols], 1, 1)
+                    grad_near(m, c, zd, xd).wait()
+            for k in range(chunk_width // step_width):
+                cols = columns(c * chunk_width + k * step_width, step_width)
+                piece = jnp.concatenate(
+                    [gall[m, j, :, cols].astype(wide) for j in range(tp_count)], 0
+                ).astype(low)
+                up_ref[m, :, cols] = piece
+                total = total + contract(piece, wo[:, cols], 1, 1)
+            return total
 
         grad_heads[...] = lax.fori_loop(
-            0, width // step_width, upstream, jnp.zeros((tokens, head_cols), wide)
+            0, CHUNKS, upstream, jnp.zeros((tokens, head_cols), wide)
         ).astype(low)
         grad_keys = jnp.zeros((tokens, HEAD_WIDTH), wide)
         grad_values = jnp.zeros((tokens, HEAD_WIDTH), wide)
@@ -565,7 +579,6 @@
             key_copy(m, d).wait()
 
         dots = jnp.zeros((rows, 1), wide)
-        chunk = 1024
         for k in range(tp_count):
             cols = slice(k * slice_width, (k + 1) * slice_width)
             normed_grad = key_recv[m, k].astype(wide) + jnp.sum(
@@ -580,17 +593,17 @@
             dots = dots + jnp.sum(scaled * unit_part, -1, keepdims=True)
         dots = dots / width
         inv = inverse[m, :, 0:1]
-        for k in range(width // chunk):
-            cols = slice(k * chunk, (k + 1) * chunk)
+        for c in range(CHUNKS):
+            cols = slice(c * chunk_width, (c + 1) * chunk_width)
             gin_ref[m, :, cols] = (
                 gall[m, me, :, cols].astype(wide)
                 + inv * (grad_unit[:, cols] - unit[m, :, cols] * dots)
             ).astype(low)
 
-        @pl.when(feeds)
-        def _():
-            for zd in range(outer):
-                hop(m, zd, sec - 1).start()
+            @pl.when(feeds)
+            def _():
+                for zd in range(outer):
+                    hop(m, c, zd, sec - 1).start()
 
         return carry
 
@@ -619,8 +632,9 @@
     @pl.when(feeds)
     def _():
         for m in range(batch_groups):
-            for zd in range(outer):
-                hop(m, zd, sec - 1).wait_send()
+            for c in range(CHUNKS):
+                for zd in range(outer):
+                    hop(m, c, zd, sec - 1).wait_send()
 
 
 def relay(saved, gain, wq, kw, vw, wo, direction, ratio, ids, slots, counts):
@@ -635,7 +649,7 @@
     key_count = key_width // HEAD_WIDTH
     slice_width = kw.shape[0]
     vmem = pl.BlockSpec(memory_space=pltpu.VMEM)
-    hbm = pl.BlockSpec(memory_space=pl.ANY)
+    hbm = pl.BlockSpec(memory_space=pltpu.HBM)
     dma = pltpu.SemaphoreType.DMA
     groups = batch_groups
     return pl.pallas_call(
@@ -650,12 +664,10 @@
             jax.ShapeDtypeStruct((2, groups, tokens, key_width), low),
             jax.ShapeDtypeStruct((1, width), wide),
         ],
-        in_specs=[vmem, vmem, hbm, hbm, hbm, hbm] + [vmem] * 5,
+        in_specs=[vmem, vmem, hbm, vmem, vmem, hbm, vmem] + [vmem] * 4,
         out_specs=[vmem] * 8,
         scratch_shapes=[
             pltpu.VMEM(wq.shape, low),
-            pltpu.VMEM(kw.shape, low),
-            pltpu.VMEM(vw.shape, low),
             pltpu.VMEM(wo.shape, low),
             pltpu.VMEM((tp_count, groups, rows, width), low),
             pltpu.VMEM((groups, tp_count, rows, width), low),
@@ -679,18 +691,18 @@
             pltpu.VMEM((groups, outer, 2, tokens, HEAD_WIDTH), low),
             pltpu.VMEM((tp_count, 8, LANES), wide),
             pltpu.VMEM((tp_count, 1, width), wide),
-            dma((4,)),
+            dma((2,)),
             dma((tp_count,)),
             dma((tp_count,)),
-            dma((outer,)),
-            dma((outer,)),
-            dma((tp_count,)),
-            dma((tp_count,)),
-            dma((groups, outer)),
-            dma((groups, outer)),
-            dma((groups, tp_count)),
-            dma((groups, tp_count)),
-            dma((groups, outer)),
+            dma((CHUNKS, outer)),
+            dma((CHUNKS, outer)),
+            dma((CHUNKS, tp_count)),
+            dma((CHUNKS, tp_count)),
+            dma((groups, CHUNKS, outer)),
+            dma((groups, CHUNKS, outer)),
+            dma((groups, CHUNKS, tp_count)),
+            dma((groups, CHUNKS, tp_count)),
+            dma((groups, CHUNKS, outer)),
             dma((outer,)),
             dma((outer,)),
             dma((inner,)),
@@ -732,15 +744,20 @@
     of_out,
     gain_out,
 ):
-    @pl.when(pl.program_id(0) == 0)
+    step = pl.program_id(0)
+
+    @pl.when(step == 0)
     def _():
         grads_out[...] = grads_in[...]
         gain_out[...] = gain_in[...]
 
-    of_query[...] = contract(normed_ref[...], gq_ref[...], 0, 0).astype(low)
-    of_out[...] = contract(att_ref[...], up_ref[...], 0, 0).astype(low)
-    of_key[...] = contract(normed_cols_ref[...], dkv_ref[0], 0, 0).astype(low)
-    of_value[...] = contract(normed_cols_ref[...], dkv_ref[1], 0, 0).astype(low)
+    part, narrow = of_query.shape[0], of_key.shape[0]
+    cols = pl.ds(pl.multiple_of(step * part, part), part)
+    own = normed_cols_ref[:, pl.ds(pl.multiple_of(step * narrow, narrow), narrow)]
+    of_query[...] = contract(normed_ref[:, cols], gq_ref[...], 0, 0).astype(low)
+    of_out[...] = contract(att_ref[...], up_ref[:, cols], 0, 0).astype(low)
+    of_key[...] = contract(own, dkv_ref[0], 0, 0).astype(low)
+    of_value[...] = contract(own, dkv_ref[1], 0, 0).astype(low)
 
 
 def weight_gradients(normed, normed_cols, grad_queries, dkv, attended, upstream, grads, gain):
@@ -770,16 +787,7 @@
             jax.ShapeDtypeStruct((head_cols, width), low),
             jax.ShapeDtypeStruct(gain.shape, wide),
         ],
-        in_specs=[
-            lanes((every, part)),
-            lanes((every, HEAD_WIDTH)),
-            whole(grad_queries.shape),
-            whole(dkv.shape),
-            whole(attended.shape),
-            lanes((every, part)),
-            whole(grads.shape),
-            whole(gain.shape),
-        ],
+        in_specs=[pl.BlockSpec(memory_space=pltpu.VMEM)] * 8,
         out_specs=[
             whole(grads.shape),
             above((part, head_cols)),

time: 261 us -> 239 us (0.916)
  Pallas kernels: 250 us -> 227 us
    pallas_call x1, Pallas kernels: 241 us -> 219 us  [relay(): pl.pallas_call(functools.partial(relay_kernel, lax.axis_size('section'),...]
    unnamed x17 -> x19, local copies, waits for them, and re-layouts: 9.93 us -> 11.3 us
where the time goes in v2:
time: 239 us
  Pallas kernels  227 us (95%)
  local copies, waits for them, and re-layouts  11.3 us (5%)
    pallas_call x1, Pallas kernels, relay(): pl.pallas_call(functools.partial(relay_kernel, lax.axis_size('section'),...  219 us
    unnamed x19, local copies, waits for them, and re-layouts  11.3 us
    pallas_call x1, Pallas kernels, weight_gradients(): pl.pallas_call(weights_kernel, grid=(steps,), out_shape=[jax.ShapeDtypeSt...  8.21 us

profile of v2, /device:TPU:0, one launch (start us, length us, event | category | flops | bytes accessed | tf_op | source)
XLA Modules:
  0.0 238.7 jit_solution(7619791789732181533)
XLA Ops:
  0.6 0.8 copy.17.counts_ref
  1.4 0.0 copy-start
  1.4 3.4 %copy-done = bf16[1,8192,512]{2,1,0:T(8,128)(2,1)S(1)} copy-done((bf16[1,8192,512]{2,1,0:T(8,128)(2,1)S(1)}, bf16[1,8192,512]{2,1,0:T(8,128)(2,1)}, u32[]{:S(2)}) %copy-start) | copy-done | bytes 8388632
  4.8 0.0 copy-start.1
  4.8 1.2 copy-done.1
  6.0 0.0 copy-start.2
  6.0 1.2 copy-done.2
  7.2 0.0 copy-start.3
  7.2 0.9 copy-done.3
  8.2 0.0 copy-start.4
  8.2 0.9 copy-done.4
  9.1 0.0 copy-start.5
  9.1 0.8 copy-done.5
  9.9 0.0 copy-start.6
  9.9 0.7 copy-done.6
  10.6 0.0 copy-start.7
  10.6 0.7 copy-done.7
  11.2 0.0 copy-start.8
  11.2 0.7 copy-done.8
  11.9 218.6 %relay.1 = (bf16[2,8,8192]{2,1,0:T(8,128)(2,1)S(1)}, bf16[2,64,8192]{2,1,0:T(8,128)(2,1)S(1)}, bf16[128,8192]{1,0:T(8,128)(2,1)S(1)}, bf16[128,1024]{1,0:T(8,128...) custom-call(bf16[2,8,8192]{2,1,0:T(8,128)(2,1)S(1)} %bitcast.17, ...), custom_call_target="tpu_custom_call" | custom-call | tf_op jit(solution)/shard_map/relay/pallas_call | solution.py:655
  230.5 8.2 %weight_gradients.1 = (bf16[2,8,8192]{2,1,0:T(8,128)(2,1)}, bf16[8192,512]{1,0:T(8,128)(2,1)}, bf16[1024,512]{1,0:T(8,128)(2,1)}, bf16[1024,512]{1,0:T(8,128)(2,...) custom-call(bf16[128,8192]{1,0:T(8,128)(2,1)S(1)} %get-tuple-element.20.normed_ref, ...), custom_call_target="tpu_custom_call" | custom-call | tf_op jit(solution)/shard_map/weight_gradients/pallas_call | solution.py:779
Async XLA Ops:
  1.4 3.4 %copy-start = (bf16[1,8192,512]{2,1,0:T(8,128)(2,1)S(1)}, bf16[1,8192,512]{2,1,0:T(8,128)(2,1)}, u32[]{:S(2)}) copy-start(bf16[1,8192,512]{2,1,0:T(8,128)(2,1)} %param.13) | copy-start | bytes 25165828
  4.8 1.2 copy-start.1
  6.0 1.2 copy-start.2
  7.2 0.9 copy-start.3
  8.2 0.9 copy-start.4
  9.1 0.8 copy-start.5
  9.9 0.7 copy-start.6
  10.6 0.7 copy-start.7
  11.2 0.7 copy-start.8

commit v3 on v2

--- a/solution.py
+++ b/solution.py
@@ -18,7 +18,7 @@
 masked_score = -1e30
 
 MESH = pl.DeviceIdType.MESH
-VMEM_LIMIT = 38 * 1024 * 1024
+VMEM_LIMIT = 56 * 1024 * 1024
 low, wide = jnp.bfloat16, jnp.float32
 
 
@@ -38,28 +38,35 @@
 def relay_kernel(
     section_count,
     tp_count,
-    saved_ref,
+    saved_hbm,
     gain_ref,
     wq_hbm,
-    kw,
-    vw,
+    kw_hbm,
+    vw_hbm,
     wo_hbm,
-    dir_ref,
+    dir_hbm,
     ratio_ref,
     ids_ref,
     slot_ref,
     counts_ref,
     gin_ref,
-    up_ref,
-    normed_ref,
+    up_hbm,
+    normed_hbm,
     normed_cols_ref,
     att_ref,
     gq_ref,
     dkv_ref,
     gain_out_ref,
+    saved_ref,
+    dir_ref,
+    kw,
+    vw,
     wq,
     wo,
+    up_ref,
+    normed_ref,
     nall,
+    top,
     gall,
     part,
     near_recv,
@@ -82,13 +89,19 @@
     sums_all,
     gain_all,
     w_sem,
+    o_sem,
     s_send,
     s_recv,
     nf_send,
     nf_recv,
     nn_send,
     nn_recv,
-    gf_send,
+    tf_send,
+    tf_recv,
+    tn_send,
+    tn_recv,
+    ty_send,
+    ty_recv,
     gf_recv,
     gn_send,
     gn_recv,
@@ -125,13 +138,15 @@
     key_count = key_width // HEAD_WIDTH
     sharers = tp_count // key_count
     group_width = inner * slice_width
-    step_width = min(1024, group_width)
+    step_width = min(2048, group_width)
+    merge_width = min(1024, width)
     chunk_width = width // CHUNKS
     per_group = CHUNKS // batch_groups
     normed_width = width // per_group
     scale = 1.0 / math.sqrt(HEAD_WIDTH)
     is_last = sec == section_count - 1
     feeds = sec > 0
+    helps = sec == section_count - 3
 
     def zpeer(zd):
         return lax.rem(z + zd, outer)
@@ -161,7 +176,14 @@
     loads = [
         pltpu.make_async_copy(source, target, w_sem.at[i])
         for i, (source, target) in enumerate(
-            ((wq_hbm, wq), (wo_hbm, wo))
+            (
+                (saved_hbm, saved_ref),
+                (dir_hbm, dir_ref),
+                (kw_hbm, kw),
+                (vw_hbm, vw),
+                (wq_hbm, wq),
+                (wo_hbm, wo),
+            )
         )
     ]
     for load in loads:
@@ -180,6 +202,11 @@
                 barrier, inc=1, device_id=(sec + 1, zpeer(zd) * inner + x), device_id_type=MESH
             )
 
+    @pl.when(is_last)
+    def _():
+        pl.semaphore_signal(barrier, inc=1, device_id=(sec - 2, me), device_id_type=MESH)
+
+    loads[0].wait()
     gain_row = gain_ref[...].astype(wide)
     for m in range(batch_groups):
         rows_in = saved_ref[m].astype(wide)
@@ -189,7 +216,11 @@
         unit[m] = unit_rows
         nall[me, m] = (unit_rows * gain_row).astype(low)
 
-    @pl.when(feeds)
+    @pl.when(helps)
+    def _():
+        pl.semaphore_wait(barrier, tp_count + outer)
+
+    @pl.when(feeds & jnp.logical_not(helps))
     def _():
         pl.semaphore_wait(barrier, tp_count - 1 + outer)
 
@@ -241,8 +272,23 @@
         return columns(c * chunk_width, chunk_width)
 
     def top_far(m, c, zd):
-        block = gall.at[m, me, :, chunk(c)]
-        return far(block, block, gf_send.at[m, c, zd], gf_recv.at[m, c, zd], zd)
+        block = top.at[m, me, :, chunk(c)]
+        return far(block, block, tf_send.at[m, c, zd], tf_recv.at[m, c, zd], zd)
+
+    def top_near(m, c, zd, xd):
+        block = top.at[m, block_from(zd), :, chunk(c)]
+        slot = zd * inner + xd
+        return near(block, block, tn_send.at[m, c, slot], tn_recv.at[m, c, slot], xd)
+
+    def top_move(m, c, section):
+        return remote(
+            top.at[m, :, :, chunk(c)],
+            gall.at[m, :, :, chunk(c)],
+            ty_send.at[m, c],
+            ty_recv.at[m, c],
+            section,
+            me,
+        )
 
     def hop(m, c, zd, section):
         return remote(
@@ -259,14 +305,9 @@
         slot = zd * inner + xd
         return near(block, block, gn_send.at[m, c, slot], gn_recv.at[m, c, slot], xd)
 
-    def top_forward(m):
-        for c in range(CHUNKS):
-            for zd in range(1, outer):
-                top_far(m, c, zd).wait()
-                for xd in range(1, inner):
-                    grad_near(m, c, zd, xd).start()
-
-    @pl.when(is_last)
+    loads[1].wait()
+
+    @pl.when(helps)
     def _():
         sums_all[me] = jnp.zeros(sums_all.shape[1:], wide)
         for m in range(batch_groups):
@@ -278,24 +319,7 @@
         for d in range(1, tp_count):
             sums_copy(d).start()
 
-    @pl.when(sec == section_count - 2)
-    def _():
-        pl.semaphore_wait(go, 1)
-
-    for c in range(CHUNKS):
-        for zd in range(1, outer):
-            normed_far(c, zd).start()
-        for xd in range(1, inner):
-            normed_near(c, 0, xd).start()
-
-    def top_start(m):
-        for c in range(CHUNKS):
-            for zd in range(1, outer):
-                top_far(m, c, zd).start()
-            for xd in range(1, inner):
-                grad_near(m, c, 0, xd).start()
-
-    @pl.when(is_last)
+    @pl.when(helps)
     def _():
         for d in range(1, tp_count):
             sums_copy(d).wait()
@@ -314,8 +338,45 @@
                 -1,
                 keepdims=True,
             )
-            gall[m, me] = (token_weight * dir_ref[m].astype(wide)).astype(low)
-        top_start(0)
+            top[m, me] = (token_weight * dir_ref[m].astype(wide)).astype(low)
+            for c in range(CHUNKS):
+                for zd in range(1, outer):
+                    top_far(m, c, zd).start()
+                for xd in range(1, inner):
+                    top_near(m, c, 0, xd).start()
+
+    @pl.when(helps)
+    def _():
+        order = [(m, c) for m in range(batch_groups) for c in range(CHUNKS)]
+
+        def top_forward(m, c):
+            for zd in range(1, outer):
+                top_far(m, c, zd).wait()
+                for xd in range(1, inner):
+                    top_near(m, c, zd, xd).start()
+
+        top_forward(*order[0])
+        for at, (m, c) in enumerate(order):
+            if at + 1 < len(order):
+                top_forward(*order[at + 1])
+            for zd in range(outer):
+                for xd in range(1, inner):
+                    top_near(m, c, zd, xd).wait()
+            top_move(m, c, sec + 2).start()
+
+        @pl.when(feeds)
+        def _():
+            pl.semaphore_signal(go, inc=1, device_id=(sec - 1, me), device_id_type=MESH)
+
+    @pl.when((sec == section_count - 2) | (sec == section_count - 4))
+    def _():
+        pl.semaphore_wait(go, 1)
+
+    for c in range(CHUNKS):
+        for zd in range(1, outer):
+            normed_far(c, zd).start()
+        for xd in range(1, inner):
+            normed_near(c, 0, xd).start()
 
     for c in range(CHUNKS):
         for zd in range(1, outer):
@@ -329,20 +390,26 @@
 
     @pl.when(is_last)
     def _():
-        top_forward(0)
         pl.semaphore_signal(go, inc=1, device_id=(sec - 1, me), device_id_type=MESH)
 
     def merge(k, carry):
-        cols = columns(k * step_width, step_width)
+        cols = columns(k * merge_width, merge_width)
         for m in range(batch_groups):
             normed_ref[m * tokens : (m + 1) * tokens, cols] = jnp.concatenate(
                 [nall[j, m, :, cols].astype(wide) for j in range(tp_count)], 0
             ).astype(low)
         return carry
 
-    lax.fori_loop(0, width // step_width, merge, 0)
+    lax.fori_loop(0, width // merge_width, merge, 0)
+    normed_out = pltpu.make_async_copy(normed_ref, normed_hbm, o_sem.at[0])
+    normed_out.start()
+
+    def up_out(m):
+        return pltpu.make_async_copy(up_ref.at[m], up_hbm.at[m], o_sem.at[1 + m])
 
     normed_cols_ref[...] = normed_ref[:, columns(me * slice_width, slice_width)]
+    loads[2].wait()
+    loads[3].wait()
     for kind, weight_ref in enumerate((kw, vw)):
         product = jnp.dot(normed_cols_ref[...], weight_ref[...], preferred_element_type=wide)
         for k in range(key_count):
@@ -358,7 +425,7 @@
     for zd in range(1, outer):
         kv_far_copy(zd).start()
 
-    loads[0].wait()
+    loads[4].wait()
 
     def project(k, total):
         cols = columns(k * step_width, step_width)
@@ -381,12 +448,6 @@
         kv_near_copy(xd).start()
     for xd in range(1, inner):
         kv_near_copy(xd).wait()
-
-    @pl.when(is_last)
-    def _():
-        for m in range(1, batch_groups):
-            top_start(m)
-
     for kind in range(2):
         total = kv_near[0, kind].astype(wide)
         for xd in range(1, inner):
@@ -409,13 +470,8 @@
             att_ref[m * tokens : (m + 1) * tokens, head] = jnp.dot(
                 value.astype(low), kv[m, 1], preferred_element_type=wide
             ).astype(low)
-    loads[1].wait()
+    loads[5].wait()
     gain_out_ref[...] = jnp.zeros_like(gain_out_ref)
-
-    @pl.when(is_last)
-    def _():
-        for m in range(1, batch_groups):
-            top_forward(m)
 
     def dkv_near_copy(m, xd):
         return near(
@@ -485,7 +541,7 @@
             else:
                 far_recv[m, 0, :, cols] = total.astype(low)
 
-    def step(m, carry):
+    def begin(m):
         def forward(c):
             @pl.when(jnp.logical_not(is_last))
             def _():
@@ -498,9 +554,17 @@
 
         def upstream(c, total):
             pl.when(c + 1 < CHUNKS)(functools.partial(forward, c + 1))
-            for zd in range(outer):
-                for xd in range(1, inner):
-                    grad_near(m, c, zd, xd).wait()
+
+            @pl.when(is_last)
+            def _():
+                top_move(m, c, sec).wait_recv()
+
+            @pl.when(jnp.logical_not(is_last))
+            def _():
+                for zd in range(outer):
+                    for xd in range(1, inner):
+                        grad_near(m, c, zd, xd).wait()
+
             for k in range(chunk_width // step_width):
                 cols = columns(c * chunk_width + k * step_width, step_width)
                 piece = jnp.concatenate(
@@ -513,6 +577,7 @@
         grad_heads[...] = lax.fori_loop(
             0, CHUNKS, upstream, jnp.zeros((tokens, head_cols), wide)
         ).astype(low)
+        up_out(m).start()
         grad_keys = jnp.zeros((tokens, HEAD_WIDTH), wide)
         grad_values = jnp.zeros((tokens, HEAD_WIDTH), wide)
         for h in range(local_heads):
@@ -532,6 +597,7 @@
         for xd in range(1, inner):
             dkv_near_copy(m, xd).start()
 
+    def spread(m):
         part_group(m, 1)
 
         for xd in range(1, inner):
@@ -570,6 +636,7 @@
         key_recv[m, me] = key_send[m, me]
         sum_group(m, outer)
 
+    def finish(m):
         for zd in range(1, outer):
             for i in range(1, outer + 1):
                 part_far(m, i, lax.rem(z + i, outer), zd).wait_send()
@@ -605,9 +672,14 @@
                 for zd in range(outer):
                     hop(m, c, zd, sec - 1).start()
 
-        return carry
-
-    lax.fori_loop(0, batch_groups, step, 0)
+    begin(0)
+    for m in range(batch_groups):
+        spread(m)
+        if m + 1 < batch_groups:
+            pl.when(is_last)(functools.partial(begin, m + 1))
+        finish(m)
+        if m + 1 < batch_groups:
+            pl.when(jnp.logical_not(is_last))(functools.partial(begin, m + 1))
 
     def gain_copy(d):
         return remote(
@@ -628,6 +700,15 @@
     for d in range(1, tp_count):
         total = total + gain_all[d]
     gain_out_ref[...] = total
+    normed_out.wait()
+    for m in range(batch_groups):
+        up_out(m).wait()
+
+    @pl.when(helps)
+    def _():
+        for m in range(batch_groups):
+            for c in range(CHUNKS):
+                top_move(m, c, sec + 2).wait_send()
 
     @pl.when(feeds)
     def _():
@@ -664,12 +745,19 @@
             jax.ShapeDtypeStruct((2, groups, tokens, key_width), low),
             jax.ShapeDtypeStruct((1, width), wide),
         ],
-        in_specs=[vmem, vmem, hbm, vmem, vmem, hbm, vmem] + [vmem] * 4,
-        out_specs=[vmem] * 8,
+        in_specs=[hbm, vmem, hbm, hbm, hbm, hbm, hbm] + [vmem] * 4,
+        out_specs=[vmem, hbm, hbm] + [vmem] * 5,
         scratch_shapes=[
+            pltpu.VMEM(saved.shape, low),
+            pltpu.VMEM(direction.shape, low),
+            pltpu.VMEM(kw.shape, low),
+            pltpu.VMEM(vw.shape, low),
             pltpu.VMEM(wq.shape, low),
             pltpu.VMEM(wo.shape, low),
+            pltpu.VMEM((groups, tokens, width), low),
+            pltpu.VMEM((every, width), low),
             pltpu.VMEM((tp_count, groups, rows, width), low),
+            pltpu.VMEM((groups, tp_count, rows, width), low),
             pltpu.VMEM((groups, tp_count, rows, width), low),
             pltpu.VMEM((groups, inner, outer, rows, width), low),
             pltpu.VMEM((groups, inner - 1, outer, rows, width), low),
@@ -691,7 +779,8 @@
             pltpu.VMEM((groups, outer, 2, tokens, HEAD_WIDTH), low),
             pltpu.VMEM((tp_count, 8, LANES), wide),
             pltpu.VMEM((tp_count, 1, width), wide),
-            dma((2,)),
+            dma((6,)),
+            dma((1 + groups,)),
             dma((tp_count,)),
             dma((tp_count,)),
             dma((CHUNKS, outer)),
@@ -699,6 +788,11 @@
             dma((CHUNKS, tp_count)),
             dma((CHUNKS, tp_count)),
             dma((groups, CHUNKS, outer)),
+            dma((groups, CHUNKS, outer)),
+            dma((groups, CHUNKS, tp_count)),
+            dma((groups, CHUNKS, tp_count)),
+            dma((groups, CHUNKS)),
+            dma((groups, CHUNKS)),
             dma((groups, CHUNKS, outer)),
             dma((groups, CHUNKS, tp_count)),
             dma((groups, CHUNKS, tp_count)),
@@ -751,11 +845,10 @@
         grads_out[...] = grads_in[...]
         gain_out[...] = gain_in[...]
 
-    part, narrow = of_query.shape[0], of_key.shape[0]
-    cols = pl.ds(pl.multiple_of(step * part, part), part)
+    narrow = of_key.shape[0]
     own = normed_cols_ref[:, pl.ds(pl.multiple_of(step * narrow, narrow), narrow)]
-    of_query[...] = contract(normed_ref[:, cols], gq_ref[...], 0, 0).astype(low)
-    of_out[...] = contract(att_ref[...], up_ref[:, cols], 0, 0).astype(low)
+    of_query[...] = contract(normed_ref[...], gq_ref[...], 0, 0).astype(low)
+    of_out[...] = contract(att_ref[...], up_ref[...], 0, 0).astype(low)
     of_key[...] = contract(own, dkv_ref[0], 0, 0).astype(low)
     of_value[...] = contract(own, dkv_ref[1], 0, 0).astype(low)
 
@@ -787,7 +880,16 @@
             jax.ShapeDtypeStruct((head_cols, width), low),
             jax.ShapeDtypeStruct(gain.shape, wide),
         ],
-        in_specs=[pl.BlockSpec(memory_space=pltpu.VMEM)] * 8,
+        in_specs=[
+            lanes((every, part)),
+            whole(normed_cols.shape),
+            whole(grad_queries.shape),
+            whole(dkv.shape),
+            whole(attended.shape),
+            lanes((every, part)),
+            whole(grads.shape),
+            whole(gain.shape),
+        ],
         out_specs=[
             whole(grads.shape),
             above((part, head_cols)),
@@ -796,7 +898,7 @@
             lanes((head_cols, part)),
             whole(gain.shape),
         ],
-        compiler_params=pltpu.CompilerParams(vmem_limit_bytes=32 * 1024 * 1024),
+        compiler_params=pltpu.CompilerParams(vmem_limit_bytes=VMEM_LIMIT),
         name="weight_gradients",
     )(normed, normed_cols, grad_queries, dkv, attended, upstream, grads, gain)
 

time: 239 us -> 220 us (0.921)
  Pallas kernels: 227 us -> 217 us
  local copies, waits for them, and re-layouts: 11.3 us -> 1.35 us
    pallas_call x1, Pallas kernels: 219 us -> 206 us  [relay(): pl.pallas_call(functools.partial(relay_kernel, lax.axis_size('section'),...]
    unnamed x19 -> x1, local copies, waits for them, and re-layouts: 11.3 us -> 1.35 us
    pallas_call x1, Pallas kernels: 8.21 us -> 11.1 us  [weight_gradients(): pl.pallas_call(weights_kernel, grid=(steps,), out_shape=[jax.ShapeDtypeSt...]
where the time goes in v3:
time: 220 us; the launch traced here: 219 us
  Pallas kernels  217 us (99%)
    pallas_call x1, Pallas kernels, relay(): pl.pallas_call(functools.partial(relay_kernel, lax.axis_size('section'),...  206 us
    pallas_call x1, Pallas kernels, weight_gradients(): pl.pallas_call(weights_kernel, grid=(steps,), out_shape=[jax.ShapeDtypeSt...  11.1 us

profile of v3, /device:TPU:0, one launch (start us, length us, event | category | flops | bytes accessed | tf_op | source)
XLA Modules:
  0.0 219.2 jit_solution(12005873095493994062)
XLA Ops:
  0.6 1.3 copy.17.counts_ref
  2.0 206.2 %relay.1 = (bf16[2,8,8192]{2,1,0:T(8,128)(2,1)}, bf16[2,64,8192]{2,1,0:T(8,128)(2,1)}, bf16[128,8192]{1,0:T(8,128)(2,1)}, bf16[128,1024]{1,0:T(8,128)(2,1)}, bf1...) custom-call(bf16[2,8,8192]{2,1,0:T(8,128)(2,1)} %bitcast.18, ...), custom_call_target="tpu_custom_call" | custom-call | tf_op jit(solution)/shard_map/relay/pallas_call | solution.py:736
  208.2 11.1 %weight_gradients.1 = (bf16[2,8,8192]{2,1,0:T(8,128)(2,1)}, bf16[8192,512]{1,0:T(8,128)(2,1)}, bf16[1024,512]{1,0:T(8,128)(2,1)}, bf16[1024,512]{1,0:T(8,128)(2,...) custom-call(bf16[128,8192]{1,0:T(8,128)(2,1)} %get-tuple-element.20.normed_ref, ...), custom_call_target="tpu_custom_call" | custom-call | tf_op jit(solution)/shard_map/weight_gradients/pallas_call | solution.py:872

commit v4 on v3

--- a/solution.py
+++ b/solution.py
@@ -242,9 +242,9 @@
         return (own == slot.astype(wide)).astype(wide)
 
     def slot_counts(m, kind):
-        pairs = counts_ref.shape[0]
+        pairs = counts_ref.shape[1]
         table = iota((pairs, SLOTS), 0) == jnp.broadcast_to(slot_ref[m : m + 1], (pairs, SLOTS))
-        count = counts_ref[:, kind : kind + 1].astype(wide)
+        count = to_column(counts_ref[kind : kind + 1].astype(wide), pairs, 0)
         return jnp.sum(jnp.where(table, count, 0.0), 0, keepdims=True)
 
     def sums_copy(d):
@@ -541,19 +541,18 @@
             else:
                 far_recv[m, 0, :, cols] = total.astype(low)
 
+    def forward(m, c):
+        @pl.when(jnp.logical_not(is_last))
+        def _():
+            for zd in range(outer):
+                hop(m, c, zd, sec).wait_recv()
+                for xd in range(1, inner):
+                    grad_near(m, c, zd, xd).start()
+
     def begin(m):
-        def forward(c):
-            @pl.when(jnp.logical_not(is_last))
-            def _():
-                for zd in range(outer):
-                    hop(m, c, zd, sec).wait_recv()
-                    for xd in range(1, inner):
-                        grad_near(m, c, zd, xd).start()
-
-        forward(0)
-
         def upstream(c, total):
-            pl.when(c + 1 < CHUNKS)(functools.partial(forward, c + 1))
+            if m == 0:
+                pl.when(c + 1 < CHUNKS)(functools.partial(forward, m, c + 1))
 
             @pl.when(is_last)
             def _():
@@ -636,6 +635,16 @@
         key_recv[m, me] = key_send[m, me]
         sum_group(m, outer)
 
+    def gain_copy(d):
+        return remote(
+            gain_all.at[me],
+            gain_all.at[me],
+            t_send.at[d],
+            t_recv.at[d],
+            sec,
+            lax.rem(me + d, tp_count),
+        )
+
     def finish(m):
         for zd in range(1, outer):
             for i in range(1, outer + 1):
@@ -645,7 +654,7 @@
         for d in range(1, tp_count):
             key_copy(m, d).wait()
 
-        dots = jnp.zeros((rows, 1), wide)
+        products = jnp.zeros((rows, slice_width), wide)
         for k in range(tp_count):
             cols = slice(k * slice_width, (k + 1) * slice_width)
             normed_grad = key_recv[m, k].astype(wide) + jnp.sum(
@@ -657,8 +666,12 @@
             )
             scaled = normed_grad * gain_ref[:, cols].astype(wide)
             grad_unit[:, cols] = scaled
-            dots = dots + jnp.sum(scaled * unit_part, -1, keepdims=True)
-        dots = dots / width
+            products = products + scaled * unit_part
+        if m + 1 == batch_groups:
+            gain_all[me] = gain_out_ref[...].astype(low)
+            for d in range(1, tp_count):
+                gain_copy(d).start()
+        dots = jnp.sum(products, -1, keepdims=True) / width
         inv = inverse[m, :, 0:1]
         for c in range(CHUNKS):
             cols = slice(c * chunk_width, (c + 1) * chunk_width)
@@ -672,33 +685,24 @@
                 for zd in range(outer):
                     hop(m, c, zd, sec - 1).start()
 
+    forward(0, 0)
     begin(0)
     for m in range(batch_groups):
         spread(m)
+        if m + 1 < batch_groups:
+            for c in range(CHUNKS):
+                forward(m + 1, c)
         if m + 1 < batch_groups:
             pl.when(is_last)(functools.partial(begin, m + 1))
         finish(m)
         if m + 1 < batch_groups:
             pl.when(jnp.logical_not(is_last))(functools.partial(begin, m + 1))
 
-    def gain_copy(d):
-        return remote(
-            gain_all.at[me],
-            gain_all.at[me],
-            t_send.at[d],
-            t_recv.at[d],
-            sec,
-            lax.rem(me + d, tp_count),
-        )
-
-    gain_all[me] = gain_out_ref[...]
-    for d in range(1, tp_count):
-        gain_copy(d).start()
     for d in range(1, tp_count):
         gain_copy(d).wait()
-    total = gain_all[0]
+    total = gain_all[0].astype(wide)
     for d in range(1, tp_count):
-        total = total + gain_all[d]
+        total = total + gain_all[d].astype(wide)
     gain_out_ref[...] = total
     normed_out.wait()
     for m in range(batch_groups):
@@ -778,7 +782,7 @@
             pltpu.VMEM((groups, inner, 2, tokens, HEAD_WIDTH), low),
             pltpu.VMEM((groups, outer, 2, tokens, HEAD_WIDTH), low),
             pltpu.VMEM((tp_count, 8, LANES), wide),
-            pltpu.VMEM((tp_count, 1, width), wide),
+            pltpu.VMEM((tp_count, 1, width), low),
             dma((6,)),
             dma((1 + groups,)),
             dma((tp_count,)),
@@ -930,7 +934,7 @@
         tok_logratio,
         segment_ids,
         pair_of_slot,
-        pair_counts,
+        pair_counts.T,
     )
     grads, of_query, of_key, of_value, of_out, gain_total = weight_gradients(
         normed,

time: 220 us -> 213 us (0.968)
  Pallas kernels: 217 us -> 212 us
    pallas_call x1, Pallas kernels: 206 us -> 201 us  [relay(): pl.pallas_call(functools.partial(relay_kernel, lax.axis_size('section'),...]
where the time goes in v4:
time: 213 us
  Pallas kernels  212 us (100%)
    pallas_call x1, Pallas kernels, relay(): pl.pallas_call(functools.partial(relay_kernel, lax.axis_size('section'),...  201 us
    pallas_call x1, Pallas kernels, weight_gradients(): pl.pallas_call(weights_kernel, grid=(steps,), out_shape=[jax.ShapeDtypeSt...  11.1 us

profile of v4, /device:TPU:0, one launch (start us, length us, event | category | flops | bytes accessed | tf_op | source)
XLA Modules:
  0.0 213.0 jit_solution(483586188298947325)
XLA Ops:
  0.6 201.3 %relay.1 = (bf16[2,8,8192]{2,1,0:T(8,128)(2,1)}, bf16[2,64,8192]{2,1,0:T(8,128)(2,1)}, bf16[128,8192]{1,0:T(8,128)(2,1)}, bf16[128,1024]{1,0:T(8,128)(2,1)}, bf1...) custom-call(bf16[2,8,8192]{2,1,0:T(8,128)(2,1)} %bitcast.19, ...), custom_call_target="tpu_custom_call" | custom-call | tf_op jit(solution)/shard_map/relay/pallas_call | solution.py:740
  202.0 11.1 %weight_gradients.1 = (bf16[2,8,8192]{2,1,0:T(8,128)(2,1)}, bf16[8192,512]{1,0:T(8,128)(2,1)}, bf16[1024,512]{1,0:T(8,128)(2,1)}, bf16[1024,512]{1,0:T(8,128)(2,...) custom-call(bf16[128,8192]{1,0:T(8,128)(2,1)} %get-tuple-element.20.normed_ref, ...), custom_call_target="tpu_custom_call" | custom-call | tf_op jit(solution)/shard_map/weight_gradients/pallas_call | solution.py:876

commit v5 on v4

--- a/solution.py
+++ b/solution.py
@@ -66,6 +66,7 @@
     up_ref,
     normed_ref,
     nall,
+    slices,
     top,
     gall,
     part,
@@ -122,6 +123,8 @@
     ks_recv,
     t_send,
     t_recv,
+    sl_send,
+    sl_recv,
     go,
 ):
     sec = lax.axis_index("section")
@@ -372,42 +375,32 @@
     def _():
         pl.semaphore_wait(go, 1)
 
+    def slice_copy(d):
+        peer = lax.rem(me + d, tp_count)
+        return remote(
+            nall.at[me, :, :, columns(peer * slice_width, slice_width)],
+            slices.at[me],
+            sl_send.at[d],
+            sl_recv.at[d],
+            sec,
+            peer,
+        )
+
+    for d in range(1, tp_count):
+        slice_copy(d).start()
     for c in range(CHUNKS):
         for zd in range(1, outer):
             normed_far(c, zd).start()
         for xd in range(1, inner):
             normed_near(c, 0, xd).start()
 
-    for c in range(CHUNKS):
-        for zd in range(1, outer):
-            normed_far(c, zd).wait()
-            for xd in range(1, inner):
-                normed_near(c, zd, xd).start()
-    for c in range(CHUNKS):
-        for zd in range(outer):
-            for xd in range(1, inner):
-                normed_near(c, zd, xd).wait()
-
-    @pl.when(is_last)
-    def _():
-        pl.semaphore_signal(go, inc=1, device_id=(sec - 1, me), device_id_type=MESH)
-
-    def merge(k, carry):
-        cols = columns(k * merge_width, merge_width)
-        for m in range(batch_groups):
-            normed_ref[m * tokens : (m + 1) * tokens, cols] = jnp.concatenate(
-                [nall[j, m, :, cols].astype(wide) for j in range(tp_count)], 0
-            ).astype(low)
-        return carry
-
-    lax.fori_loop(0, width // merge_width, merge, 0)
-    normed_out = pltpu.make_async_copy(normed_ref, normed_hbm, o_sem.at[0])
-    normed_out.start()
-
-    def up_out(m):
-        return pltpu.make_async_copy(up_ref.at[m], up_hbm.at[m], o_sem.at[1 + m])
-
-    normed_cols_ref[...] = normed_ref[:, columns(me * slice_width, slice_width)]
+    for d in range(1, tp_count):
+        slice_copy(d).wait()
+    slices[me] = nall[me, :, :, columns(me * slice_width, slice_width)]
+    for m in range(batch_groups):
+        normed_cols_ref[m * tokens : (m + 1) * tokens] = jnp.concatenate(
+            [slices[j, m].astype(wide) for j in range(tp_count)], 0
+        ).astype(low)
     loads[2].wait()
     loads[3].wait()
     for kind, weight_ref in enumerate((kw, vw)):
@@ -425,18 +418,11 @@
     for zd in range(1, outer):
         kv_far_copy(zd).start()
 
-    loads[4].wait()
-
-    def project(k, total):
-        cols = columns(k * step_width, step_width)
-        return total + jnp.dot(normed_ref[:, cols], wq[cols, :], preferred_element_type=wide)
-
-    product = lax.fori_loop(
-        0, width // step_width, project, jnp.zeros((every, head_cols), wide)
-    ).astype(low)
-    for m in range(batch_groups):
-        queries[m] = product[m * tokens : (m + 1) * tokens]
-
+    for c in range(CHUNKS):
+        for zd in range(1, outer):
+            normed_far(c, zd).wait()
+            for xd in range(1, inner):
+                normed_near(c, zd, xd).start()
     for zd in range(1, outer):
         kv_far_copy(zd).wait()
     for kind in range(2):
@@ -446,6 +432,42 @@
         kv_near[0, kind] = total.astype(low)
     for xd in range(1, inner):
         kv_near_copy(xd).start()
+    for c in range(CHUNKS):
+        for zd in range(outer):
+            for xd in range(1, inner):
+                normed_near(c, zd, xd).wait()
+
+    @pl.when(is_last)
+    def _():
+        pl.semaphore_signal(go, inc=1, device_id=(sec - 1, me), device_id_type=MESH)
+
+    def merge(k, carry):
+        cols = columns(k * merge_width, merge_width)
+        for m in range(batch_groups):
+            normed_ref[m * tokens : (m + 1) * tokens, cols] = jnp.concatenate(
+                [nall[j, m, :, cols].astype(wide) for j in range(tp_count)], 0
+            ).astype(low)
+        return carry
+
+    lax.fori_loop(0, width // merge_width, merge, 0)
+    normed_out = pltpu.make_async_copy(normed_ref, normed_hbm, o_sem.at[0])
+    normed_out.start()
+
+    def up_out(m):
+        return pltpu.make_async_copy(up_ref.at[m], up_hbm.at[m], o_sem.at[1 + m])
+
+    loads[4].wait()
+
+    def project(k, total):
+        cols = columns(k * step_width, step_width)
+        return total + jnp.dot(normed_ref[:, cols], wq[cols, :], preferred_element_type=wide)
+
+    product = lax.fori_loop(
+        0, width // step_width, project, jnp.zeros((every, head_cols), wide)
+    ).astype(low)
+    for m in range(batch_groups):
+        queries[m] = product[m * tokens : (m + 1) * tokens]
+
     for xd in range(1, inner):
         kv_near_copy(xd).wait()
     for kind in range(2):
@@ -682,7 +704,7 @@
 
             @pl.when(feeds)
             def _():
-                for zd in range(outer):
+                for zd in (*range(1, outer), 0):
                     hop(m, c, zd, sec - 1).start()
 
     forward(0, 0)
@@ -761,6 +783,7 @@
             pltpu.VMEM((groups, tokens, width), low),
             pltpu.VMEM((every, width), low),
             pltpu.VMEM((tp_count, groups, rows, width), low),
+            pltpu.VMEM((tp_count, groups, rows, slice_width), low),
             pltpu.VMEM((groups, tp_count, rows, width), low),
             pltpu.VMEM((groups, tp_count, rows, width), low),
             pltpu.VMEM((groups, inner, outer, rows, width), low),
@@ -817,6 +840,8 @@
             dma((groups, tp_count)),
             dma((tp_count,)),
             dma((tp_count,)),
+            dma((tp_count,)),
+            dma((tp_count,)),
             pltpu.SemaphoreType.REGULAR,
         ],
         compiler_params=pltpu.CompilerParams(

time: 213 us -> 213 us (level)
  no operation moved by 1% of the time
where the time goes in v5:
time: 213 us; the launch traced here: 212 us
  Pallas kernels  212 us (100%)
    pallas_call x1, Pallas kernels, relay(): pl.pallas_call(functools.partial(relay_kernel, lax.axis_size('section'),...  201 us
    pallas_call x1, Pallas kernels, weight_gradients(): pl.pallas_call(weights_kernel, grid=(steps,), out_shape=[jax.ShapeDtypeSt...  11.1 us

profile of v5, /device:TPU:0, one launch (start us, length us, event | category | flops | bytes accessed | tf_op | source)
XLA Modules:
  0.0 212.4 jit_solution(16796109621813669549)
XLA Ops:
  0.6 200.7 %relay.1 = (bf16[2,8,8192]{2,1,0:T(8,128)(2,1)}, bf16[2,64,8192]{2,1,0:T(8,128)(2,1)}, bf16[128,8192]{1,0:T(8,128)(2,1)}, bf16[128,1024]{1,0:T(8,128)(2,1)}, bf1...) custom-call(bf16[2,8,8192]{2,1,0:T(8,128)(2,1)} %bitcast.19, ...), custom_call_target="tpu_custom_call" | custom-call | tf_op jit(solution)/shard_map/relay/pallas_call | solution.py:762
  201.3 11.1 %weight_gradients.1 = (bf16[2,8,8192]{2,1,0:T(8,128)(2,1)}, bf16[8192,512]{1,0:T(8,128)(2,1)}, bf16[1024,512]{1,0:T(8,128)(2,1)}, bf16[1024,512]{1,0:T(8,128)(2,...) custom-call(bf16[128,8192]{1,0:T(8,128)(2,1)} %get-tuple-element.20.normed_ref, ...), custom_call_target="tpu_custom_call" | custom-call | tf_op jit(solution)/shard_map/weight_gradients/pallas_call | solution.py:901

commit v6 on v5

--- a/solution.py
+++ b/solution.py
@@ -670,7 +670,6 @@
     def finish(m):
         for zd in range(1, outer):
             for i in range(1, outer + 1):
-                part_far(m, i, lax.rem(z + i, outer), zd).wait_send()
                 part_far(m, i, lax.rem(z - zd + i + outer, outer), zd).wait_recv()
 
         for d in range(1, tp_count):
@@ -706,6 +705,10 @@
             def _():
                 for zd in (*range(1, outer), 0):
                     hop(m, c, zd, sec - 1).start()
+
+        for zd in range(1, outer):
+            for i in range(1, outer + 1):
+                part_far(m, i, lax.rem(z + i, outer), zd).wait_send()
 
     forward(0, 0)
     begin(0)

time: 213 us -> 213 us (level)
  no operation moved by 1% of the time
where the time goes in v6:
time: 213 us
  Pallas kernels  212 us (100%)
    pallas_call x1, Pallas kernels, relay(): pl.pallas_call(functools.partial(relay_kernel, lax.axis_size('section'),...  201 us
    pallas_call x1, Pallas kernels, weight_gradients(): pl.pallas_call(weights_kernel, grid=(steps,), out_shape=[jax.ShapeDtypeSt...  11.1 us

profile of v6, /device:TPU:0, one launch (start us, length us, event | category | flops | bytes accessed | tf_op | source)
XLA Modules:
  0.0 213.0 jit_solution(7077527340744360327)
XLA Ops:
  0.6 201.3 %relay.1 = (bf16[2,8,8192]{2,1,0:T(8,128)(2,1)}, bf16[2,64,8192]{2,1,0:T(8,128)(2,1)}, bf16[128,8192]{1,0:T(8,128)(2,1)}, bf16[128,1024]{1,0:T(8,128)(2,1)}, bf1...) custom-call(bf16[2,8,8192]{2,1,0:T(8,128)(2,1)} %bitcast.19, ...), custom_call_target="tpu_custom_call" | custom-call | tf_op jit(solution)/shard_map/relay/pallas_call | solution.py:765
  201.9 11.1 %weight_gradients.1 = (bf16[2,8,8192]{2,1,0:T(8,128)(2,1)}, bf16[8192,512]{1,0:T(8,128)(2,1)}, bf16[1024,512]{1,0:T(8,128)(2,1)}, bf16[1024,512]{1,0:T(8,128)(2,...) custom-call(bf16[128,8192]{1,0:T(8,128)(2,1)} %get-tuple-element.20.normed_ref, ...), custom_call_target="tpu_custom_call" | custom-call | tf_op jit(solution)/shard_map/weight_gradients/pallas_call | solution.py:904
